TPU v7x, 32 devices: a whole 2x2x4 slice. The times are simulated.
32 devices in a mesh: groups: 2 (over y), lon: 4 (over z), lat: 4 (over x, core).
Axes of the slice: x: 2, y: 2, z: 4, core: 2. Of those that a mesh axis runs over, the one named last changes fastest.
Arguments:
- fields: bfloat16 [768, 112, 256], P(('groups', 'lat'), 'lon'), parts along dimension 0, may hold values from -6 to 6
- norm_gains: float32 [3, 256], replicated, may hold values from 0.25 to 1.75
- lon_qkv: bfloat16 [256, 768], replicated, may hold values from -0.375 to 0.375
- lon_out: bfloat16 [256, 256], replicated, may hold values from -0.375 to 0.375
- lat_qkv: bfloat16 [256, 768], replicated, may hold values from -0.375 to 0.375
- lat_out: bfloat16 [256, 256], replicated, may hold values from -0.375 to 0.375
- logit_scales: float32 [2, 8], replicated, may hold values from 0.08 to 7.6
- conv_taps: float32 [25, 256], replicated, may hold values from -1.25 to 1.25
- mlp_in: bfloat16 [256, 2048], replicated, may hold values from -0.375 to 0.375
- mlp_down: bfloat16 [1024, 256], replicated, may hold values from -0.1875 to 0.1875
Outputs:
- mixed_grid: bfloat16 [768, 112, 256], P(('groups', 'lat'), 'lon'), parts along dimension 0
There are 2 independent parts, one for each index of `groups`. A program takes and returns all parts, laid end to end along the dimension named above; an argument that names none is the same for every part. Nothing has to cross between parts.
All inputs are finite; a program needn't handle non-finite values.
Results may differ from a plain program's by a relative error of at most 0.019.
The roundings to bfloat16 on the way count: a program that leaves them out, or rounds other values in their place, can miss the bound.
Values may be sent and summed in bfloat16 or wider, within the bound.
No kernel may reach another device: no remote copies, remote signals or barrier semaphores. Data moves between devices by JAX's collectives and lax.ppermute only.
A program may use at most 64 MiB of HBM per device.

v0:
```python
import jax
import jax.numpy as jnp
from jax import lax
from jax.sharding import PartitionSpec as P

KERNEL = 5


EPSILON = 1e-05
EINSUM_FORMS = {
    "second": ("rlf,rmf->rlm", "iwr,irq->iwq"),
    "first": ("ugv,ngv->gun", "opu,uoj->opj"),
}


def extended(x, sides, width, wrap):
    for axis, dim in sides:
        count, length = (lax.axis_size(axis), x.shape[dim])
        up = [(i, (i + 1) % count) for i in range(count if wrap else count - 1)]
        down = [(j, i) for i, j in up]
        last = lax.slice_in_dim(x, length - width, length, axis=dim)
        leading = lax.slice_in_dim(x, 0, width, axis=dim)
        before = lax.ppermute(last, axis, up)
        after = lax.ppermute(leading, axis, down)
        x = jnp.concatenate([before, x, after], axis=dim)
    return x


def layer_norm(values, gains):
    average = jnp.mean(values, -1, keepdims=True)
    centred = values - average
    spread = jnp.mean(centred * centred, -1, keepdims=True)
    return centred * lax.rsqrt(spread + EPSILON) * gains


def project(inputs, weight):
    leading = inputs.shape[:-1]
    flat = inputs.reshape(-1, inputs.shape[-1])
    return jnp.dot(flat, weight, preferred_element_type=jnp.float32).reshape(
        leading + (weight.shape[1],)
    )


def split_heads(packed, heads):
    shaped = packed.reshape(packed.shape[:-1] + (heads, packed.shape[-1] // heads))
    return jnp.moveaxis(shaped, -2, 0)


def initial_state(queries, form):
    heads, first_len, second_len, head_size = queries.shape
    if form == "second":
        batch_len, length = (first_len, second_len)
    else:
        batch_len, length = (second_len, first_len)
    return (
        jnp.full((heads, batch_len, length), -1e30, jnp.float32),
        jnp.zeros((heads, batch_len, length), jnp.float32),
        jnp.zeros((heads, batch_len, length, head_size), jnp.float32),
    )


def head_step(state, queries, keys_in, values_in, factor, form):
    running_max, running_sum, running_acc = state
    scores = (
        jnp.einsum(EINSUM_FORMS[form][0], queries, keys_in, preferred_element_type=jnp.float32)
        * factor
    )
    new_max = jnp.maximum(running_max, jnp.max(scores, -1))
    fading = jnp.exp(running_max - new_max)
    weights = jnp.exp(scores - new_max[..., None])
    running_sum = running_sum * fading + jnp.sum(weights, -1)
    running_acc = running_acc * fading[..., None] + jnp.einsum(
        EINSUM_FORMS[form][1],
        weights.astype(jnp.bfloat16),
        values_in,
        preferred_element_type=jnp.float32,
    )
    return (new_max, running_sum, running_acc)


def attend_heads(state, queries, keys_in, values_in, factors, form):

    def one_head(packed):
        return head_step(packed[0], packed[1], packed[2], packed[3], packed[4], form)

    return lax.map(one_head, (state, queries, keys_in, values_in, factors))


def finish(state, form, out_weight):
    running_max, running_sum, running_acc = state
    mixed_out = running_acc / running_sum[..., None]
    order = (1, 2, 0, 3) if form == "second" else (2, 1, 0, 3)
    mixed_out = jnp.transpose(mixed_out, order)
    mixed_out = mixed_out.reshape(mixed_out.shape[:2] + (-1,)).astype(jnp.bfloat16)
    return project(mixed_out, out_weight).astype(jnp.bfloat16)


def full_attention(normed, qkv_weight, out_weight, factors, form):
    features = normed.shape[-1]
    heads = factors.shape[0]
    qkv_all = project(normed, qkv_weight).astype(jnp.bfloat16)
    queries = split_heads(qkv_all[..., :features], heads)
    keys_in = split_heads(qkv_all[..., features : 2 * features], heads)
    values_in = split_heads(qkv_all[..., 2 * features :], heads)
    state = attend_heads(initial_state(queries, form), queries, keys_in, values_in, factors, form)
    return finish(state, form, out_weight)


def per_device(
    fields,
    norm_gains,
    lon_qkv,
    lon_out,
    lat_qkv,
    lat_out,
    logit_scales,
    conv_taps,
    mlp_in,
    mlp_down,
):
    lat_rows, lon_cols, features = fields.shape
    anchor = fields.astype(jnp.float32)
    normed = layer_norm(anchor, norm_gains[0]).astype(jnp.bfloat16)
    lon_count = lax.axis_size("lon")
    stacked = normed.reshape(lon_count, lat_rows // lon_count, lon_cols, features)
    exchanged = lax.all_to_all(stacked, "lon", split_axis=0, concat_axis=2, tiled=True)
    line_set = exchanged.reshape(exchanged.shape[1], exchanged.shape[2], features)
    mixed_out = full_attention(line_set, lon_qkv, lon_out, logit_scales[0], "second")
    lon_mix = lax.all_to_all(
        mixed_out.reshape(exchanged.shape), "lon", split_axis=2, concat_axis=0, tiled=True
    ).reshape(lat_rows, lon_cols, features)
    first_state = (anchor + lon_mix.astype(jnp.float32)).astype(jnp.bfloat16)
    first_wide = first_state.astype(jnp.float32)
    normed = layer_norm(first_wide, norm_gains[1]).astype(jnp.bfloat16)
    band_count = lax.axis_size("lat")
    stacked = normed.reshape(lat_rows, band_count, lon_cols // band_count, features)
    exchanged = lax.all_to_all(stacked, "lat", split_axis=1, concat_axis=0, tiled=True)
    line_set = exchanged.reshape(exchanged.shape[0], exchanged.shape[2], features)
    mixed_out = full_attention(line_set, lat_qkv, lat_out, logit_scales[1], "first")
    lat_mix = lax.all_to_all(
        mixed_out.reshape(exchanged.shape), "lat", split_axis=0, concat_axis=1, tiled=True
    ).reshape(lat_rows, lon_cols, features)
    second_state = (first_wide + lat_mix.astype(jnp.float32)).astype(jnp.bfloat16)
    margin = KERNEL // 2
    widened = extended(second_state, (("lon", 1),), margin, True)
    widened = extended(widened, (("lat", 0),), margin, False).astype(jnp.float32)
    smoothed = jnp.zeros((lat_rows, lon_cols, features), jnp.float32)
    for row_tap in range(KERNEL):
        for col_tap in range(KERNEL):
            smoothed = (
                smoothed
                + conv_taps[row_tap * KERNEL + col_tap]
                * widened[row_tap : row_tap + lat_rows, col_tap : col_tap + lon_cols]
            )
    normed = layer_norm(smoothed, norm_gains[2]).astype(jnp.bfloat16)
    hidden_len = mlp_down.shape[0]
    gate_up = jnp.dot(normed.reshape(-1, features), mlp_in, preferred_element_type=jnp.float32)
    hidden = (jax.nn.silu(gate_up[:, :hidden_len]) * gate_up[:, hidden_len:]).astype(jnp.bfloat16)
    update = jnp.dot(hidden, mlp_down, preferred_element_type=jnp.float32).reshape(
        lat_rows, lon_cols, features
    )
    return (second_state.astype(jnp.float32) + update).astype(jnp.bfloat16)


def solution(mesh):
    in_specs = (P(("groups", "lat"), "lon", None), P(), P(), P(), P(), P(), P(), P(), P(), P())
    out_specs = P(("groups", "lat"), "lon", None)
    return jax.shard_map(
        per_device, mesh=mesh, in_specs=in_specs, out_specs=out_specs, check_vma=False
    )
```

profile of v0, /device:TPU:0, one launch (start us, length us, event | category | flops | bytes accessed | tf_op | source)
XLA Modules:
  0.0 309.2 jit_solution(7108615203687747032)
XLA Ops:
  7.2 6.3 %all-to-all-start = ((bf16[4,24,28,256]{3,1,2,0:T(8,128)(2,1)}), bf16[4,24,28,256]{3,1,2,0:T(8,128)(2,1)}, u32[]{:S(2)}, u32[]{:S(2)}) async-start(bf16[4,24,28,256]{3,1,2,0:T(8,128)(2,1)} %copy.106), calls=%async_computation | async-start | bytes 2752512 | tf_op jit(solution)/shard_map/all_to_all | solution.py:126
  13.6 32.8 %all-to-all-done = bf16[4,24,28,256]{3,1,2,0:T(8,128)(2,1)} async-done(((bf16[4,24,28,256]{3,1,2,0:T(8,128)(2,1)}), bf16[4,24,28,256]{3,1,2,0:T(8,128)(2,1)}, u32[]{:S(2)}, u32[]{:S(2)}) %all-to-all-start) | async-done | bytes 1376288 | tf_op jit(solution)/shard_map/all_to_all | solution.py:126
  46.4 2.6 convolution_convert_fusion.1
  51.2 2.6 copy.110
  53.7 2.6 copy.109
  56.3 2.5 copy.108
  58.8 39.9 %while.24 = (s32[]{:T(128)}, f32[8,24,112]{2,1,0:T(8,128)S(1)}, f32[8,24,112,32]{2,3,1,0:T(8,128)}, bf16[8,24,112,32]{2,3,0,1:T(8,128)(2,1)}, bf16[8,24,112,32]{...) while((s32[]{:T(128)}, f32[8,24,112]{2,1,0:T(8,128)S(1)}, ...), condition=%wide.region_5.6_spmd, body=%wide.region_2.5_spmd.sunk | while | flops 40440960 | bytes 4721261 | solution.py:86
  103.1 34.7 %all_to_all.48 = bf16[1,24,112,256]{3,1,0,2:T(8,128)(2,1)S(1)} all-to-all(bf16[1,24,112,256]{3,1,0,2:T(8,128)(2,1)S(1)} %copy.116), channel_id=1, replica_groups=mesh['groups'=2,'lon'=4,'lat'=4] {'lon'}, dimensions={2} | all-to-all | bytes 2752512 | tf_op jit(solution)/shard_map/all_to_all | solution.py:129
  141.8 3.9 %all-to-all-start.2 = ((bf16[96,4,7,256]{3,0,2,1:T(8,128)(2,1)}), bf16[96,4,7,256]{3,0,2,1:T(8,128)(2,1)S(1)}, u32[]{:S(2)}, u32[]{:S(2)}) async-start(bf16[96,4,7,256]{3,0,2,1:T(8,128)(2,1)} %bitcast.182), calls=%async_computation.2 | async-start | bytes 2752512 | tf_op jit(solution)/shard_map/all_to_all | solution.py:137
  145.7 17.7 %all-to-all-done.2 = bf16[96,4,7,256]{3,0,2,1:T(8,128)(2,1)S(1)} async-done(((bf16[96,4,7,256]{3,0,2,1:T(8,128)(2,1)}), bf16[96,4,7,256]{3,0,2,1:T(8,128)(2,1)S(1)}, u32[]{:S(2)}, u32[]{:S(2)}) %all-to-all-start.2) | async-done | bytes 1376288 | tf_op jit(solution)/shard_map/all_to_all | solution.py:137
  166.8 2.5 copy.122
  169.3 2.5 copy.121
  173.5 61.0 %while.25 = (s32[]{:T(128)}, f32[8,7,384]{2,0,1:T(8,128)S(1)}, f32[8,7,384,32]{2,3,0,1:T(8,128)}, bf16[8,384,7,32]{1,3,0,2:T(8,128)(2,1)}, bf16[8,384,7,32]{1,3,...) while((s32[]{:T(128)}, f32[8,7,384]{2,0,1:T(8,128)S(1)}, ...), condition=%wide.region_11.12_spmd, body=%wide.region_8.11_spmd.sunk | while | flops 140472192 | bytes 13410937 | solution.py:86
  177.9 3.1 %fusion.119 = f32[8,7,384,32]{2,3,0,1:T(8,128)} fusion(f32[8,7,384,32]{2,3,0,1:T(8,128)} %get-tuple-element.358, s32[]{:T(128)S(6)} %copy.177, f32[7,384,384]{1,2,0:T(8,128)S(1)} %get-tuple-element.320, f32[7,384]{1,0:T(8,128)S(1)} %broadcast_maximum_fusion.3, f32[]{:T(128)} %bitcast.177, bf16[8,384,7,32]{1,3,0,2:T(8,128)(2,1)} %get-tuple-element.371, ...), kind=kOutput, calls=%fused_computation.26.clone.1 | convolution fusion | flops 69242880 | bytes 4667904 | tf_op jit(solution)/shard_map/while/body/eval_jaxpr/opu,uoj->opj/dot_general | solution.py:72
  185.5 3.1 %fusion.119 = f32[8,7,384,32]{2,3,0,1:T(8,128)} fusion(f32[8,7,384,32]{2,3,0,1:T(8,128)} %get-tuple-element.358, s32[]{:T(128)S(6)} %copy.177, f32[7,384,384]{1,2,0:T(8,128)S(1)} %get-tuple-element.320, f32[7,384]{1,0:T(8,128)S(1)} %broadcast_maximum_fusion.3, f32[]{:T(128)} %bitcast.177, bf16[8,384,7,32]{1,3,0,2:T(8,128)(2,1)} %get-tuple-element.371, ...), kind=kOutput, calls=%fused_computation.26.clone.1 | convolution fusion | flops 69242880 | bytes 4667904 | tf_op jit(solution)/shard_map/while/body/eval_jaxpr/opu,uoj->opj/dot_general | solution.py:72
  193.1 3.2 %fusion.119 = f32[8,7,384,32]{2,3,0,1:T(8,128)} fusion(f32[8,7,384,32]{2,3,0,1:T(8,128)} %get-tuple-element.358, s32[]{:T(128)S(6)} %copy.177, f32[7,384,384]{1,2,0:T(8,128)S(1)} %get-tuple-element.320, f32[7,384]{1,0:T(8,128)S(1)} %broadcast_maximum_fusion.3, f32[]{:T(128)} %bitcast.177, bf16[8,384,7,32]{1,3,0,2:T(8,128)(2,1)} %get-tuple-element.371, ...), kind=kOutput, calls=%fused_computation.26.clone.1 | convolution fusion | flops 69242880 | bytes 4667904 | tf_op jit(solution)/shard_map/while/body/eval_jaxpr/opu,uoj->opj/dot_general | solution.py:72
  197.1 2.4 multiply_reduce_fusion.3
  200.8 3.1 %fusion.119 = f32[8,7,384,32]{2,3,0,1:T(8,128)} fusion(f32[8,7,384,32]{2,3,0,1:T(8,128)} %get-tuple-element.358, s32[]{:T(128)S(6)} %copy.177, f32[7,384,384]{1,2,0:T(8,128)S(1)} %get-tuple-element.320, f32[7,384]{1,0:T(8,128)S(1)} %broadcast_maximum_fusion.3, f32[]{:T(128)} %bitcast.177, bf16[8,384,7,32]{1,3,0,2:T(8,128)(2,1)} %get-tuple-element.371, ...), kind=kOutput, calls=%fused_computation.26.clone.1 | convolution fusion | flops 69242880 | bytes 4667904 | tf_op jit(solution)/shard_map/while/body/eval_jaxpr/opu,uoj->opj/dot_general | solution.py:72
  208.4 3.1 %fusion.119 = f32[8,7,384,32]{2,3,0,1:T(8,128)} fusion(f32[8,7,384,32]{2,3,0,1:T(8,128)} %get-tuple-element.358, s32[]{:T(128)S(6)} %copy.177, f32[7,384,384]{1,2,0:T(8,128)S(1)} %get-tuple-element.320, f32[7,384]{1,0:T(8,128)S(1)} %broadcast_maximum_fusion.3, f32[]{:T(128)} %bitcast.177, bf16[8,384,7,32]{1,3,0,2:T(8,128)(2,1)} %get-tuple-element.371, ...), kind=kOutput, calls=%fused_computation.26.clone.1 | convolution fusion | flops 69242880 | bytes 4667904 | tf_op jit(solution)/shard_map/while/body/eval_jaxpr/opu,uoj->opj/dot_general | solution.py:72
  216.0 3.1 %fusion.119 = f32[8,7,384,32]{2,3,0,1:T(8,128)} fusion(f32[8,7,384,32]{2,3,0,1:T(8,128)} %get-tuple-element.358, s32[]{:T(128)S(6)} %copy.177, f32[7,384,384]{1,2,0:T(8,128)S(1)} %get-tuple-element.320, f32[7,384]{1,0:T(8,128)S(1)} %broadcast_maximum_fusion.3, f32[]{:T(128)} %bitcast.177, bf16[8,384,7,32]{1,3,0,2:T(8,128)(2,1)} %get-tuple-element.371, ...), kind=kOutput, calls=%fused_computation.26.clone.1 | convolution fusion | flops 69242880 | bytes 4667904 | tf_op jit(solution)/shard_map/while/body/eval_jaxpr/opu,uoj->opj/dot_general | solution.py:72
  223.7 3.1 %fusion.119 = f32[8,7,384,32]{2,3,0,1:T(8,128)} fusion(f32[8,7,384,32]{2,3,0,1:T(8,128)} %get-tuple-element.358, s32[]{:T(128)S(6)} %copy.177, f32[7,384,384]{1,2,0:T(8,128)S(1)} %get-tuple-element.320, f32[7,384]{1,0:T(8,128)S(1)} %broadcast_maximum_fusion.3, f32[]{:T(128)} %bitcast.177, bf16[8,384,7,32]{1,3,0,2:T(8,128)(2,1)} %get-tuple-element.371, ...), kind=kOutput, calls=%fused_computation.26.clone.1 | convolution fusion | flops 69242880 | bytes 4667904 | tf_op jit(solution)/shard_map/while/body/eval_jaxpr/opu,uoj->opj/dot_general | solution.py:72
  231.3 3.1 %fusion.119 = f32[8,7,384,32]{2,3,0,1:T(8,128)} fusion(f32[8,7,384,32]{2,3,0,1:T(8,128)} %get-tuple-element.358, s32[]{:T(128)S(6)} %copy.177, f32[7,384,384]{1,2,0:T(8,128)S(1)} %get-tuple-element.320, f32[7,384]{1,0:T(8,128)S(1)} %broadcast_maximum_fusion.3, f32[]{:T(128)} %bitcast.177, bf16[8,384,7,32]{1,3,0,2:T(8,128)(2,1)} %get-tuple-element.371, ...), kind=kOutput, calls=%fused_computation.26.clone.1 | convolution fusion | flops 69242880 | bytes 4667904 | tf_op jit(solution)/shard_map/while/body/eval_jaxpr/opu,uoj->opj/dot_general | solution.py:72
  238.1 22.5 %all_to_all.49 = bf16[384,1,7,256]{3,2,1,0:T(8,128)(2,1)S(1)} all-to-all(bf16[384,1,7,256]{3,2,1,0:T(8,128)(2,1)S(1)} %copy.129), channel_id=1, replica_groups=mesh['groups'=2,'lon'=4,'lat'=4] {'lat'}, dimensions={0} | all-to-all | bytes 2752512 | tf_op jit(solution)/shard_map/all_to_all | solution.py:140
  263.5 3.4 %collective-permute-start.1 = (bf16[96,2,256]{2,0,1:T(8,128)(2,1)S(1)}, bf16[96,2,256]{2,0,1:T(8,128)(2,1)S(1)}, u32[]{:S(2)}, u32[]{:S(2)}) collective-permute-start(bf16[96,2,256]{2,0,1:T(8,128)(2,1)S(1)} %get-tuple-element.190), channel_id=1, source_target_pairs={{4,0},{8,4},{12,8},{0,12},{5,1},{9,5},{13,9},{1,13},{6,2},{10,6},{... | collective-permute-start | bytes 294920 | tf_op jit(solution)/shard_map/ppermute | solution.py:24
  267.0 3.2 %collective-permute-done = bf16[96,2,256]{2,0,1:T(8,128)(2,1)S(1)} collective-permute-done((bf16[96,2,256]{2,0,1:T(8,128)(2,1)S(1)}, bf16[96,2,256]{2,0,1:T(8,128)(2,1)S(1)}, u32[]{:S(2)}, u32[]{:S(2)}) %collective-permute-start) | collective-permute-done | bytes 98336 | tf_op jit(solution)/shard_map/ppermute | solution.py:23
  273.0 2.6 collective-permute-done.3
  276.2 8.6 %fusion.85 = (f32[96,28]{0,1:T(8,128)S(1)}, f32[96,28,256]{2,0,1:T(8,128)S(1)}) fusion(f32[100,32,256]{2,0,1:T(8,128)S(1)} %maximum_convert_fusion, f32[256]{0:T(256)S(1)} %bitcast.218, f32[256]{0:T(256)S(1)} %bitcast.219, f32[256]{0:T(256)S(1)} %bitcast.196, f32[256]{0:T(256)S(1)} %bitcast.197, f32[256]{0:T(256)S(1)} %bitcast.198, f32[256]{0:T(256)S(1)} %bitcast.199, ...), kind=kLoop, calls=%fused_computation.142 | loop fusion | flops 34403712 | bytes 71601664 | tf_op jit(solution)/shard_map/reduce_sum | solution.py:30
  288.7 3.3 %reshape.220 = bf16[2688,256]{1,0:T(8,128)(2,1)} reshape(bf16[96,28,256]{2,1,0:T(8,128)(2,1)} %copy.132) | data formatting | bytes 2752512 | tf_op jit(solution)/shard_map/reshape | solution.py:157
  292.0 4.4 %fusion.95 = f32[2688,2048]{1,0:T(8,128)S(1)} fusion(bf16[2688,256]{1,0:T(8,128)(2,1)} %reshape.220, bf16[256,2048]{1,0:T(8,128)(2,1)S(1)} %copy-done), kind=kOutput, calls=%fused_computation.150 | convolution fusion | flops 2818572288 | bytes 24444928 | tf_op jit(solution)/shard_map/dot_general | solution.py:157
  296.4 4.3 %fusion.37 = f32[2688,256]{1,0:T(8,128)} fusion(bf16[1024,256]{1,0:T(8,128)(2,1)S(1)} %copy-done.10, f32[2688,2048]{1,0:T(8,128)S(1)} %fusion.95), kind=kOutput, calls=%fused_computation.41 | convolution fusion | flops 1425801216 | bytes 25296896 | tf_op jit(solution)/shard_map/dot_general | solution.py:159
  300.7 4.0 %reshape.221 = f32[96,28,256]{2,1,0:T(8,128)} reshape(f32[2688,256]{1,0:T(8,128)} %fusion.37) | data formatting | bytes 5505024 | tf_op jit(solution)/shard_map/reshape | solution.py:159
  304.7 4.5 %fusion.75 = bf16[96,28,256]{2,0,1:T(8,128)(2,1)} fusion(f32[96,28,256]{2,1,0:T(8,128)} %reshape.221, bf16[96,28,256]{2,0,1:T(8,128)(2,1)S(1)} %fusion.50), kind=kLoop, calls=%fused_computation.113 | loop fusion | flops 2064384 | bytes 5505024 | tf_op jit(solution)/shard_map/convert_element_type | solution.py:162
  (175 shorter events, 109.3 us)
Async XLA Ops:
  0.0 292.0 %copy-start = (bf16[256,2048]{1,0:T(8,128)(2,1)S(1)}, bf16[256,2048]{1,0:T(8,128)(2,1)}, u32[]{:S(2)}) copy-start(bf16[256,2048]{1,0:T(8,128)(2,1)} %param.22) | copy-start | bytes 3145732
  0.0 5.1 %copy-start.1 = (bf16[96,28,256]{2,0,1:T(8,128)(2,1)S(1)}, bf16[96,28,256]{2,0,1:T(8,128)(2,1)}, u32[]{:S(2)}) copy-start(bf16[96,28,256]{2,0,1:T(8,128)(2,1)} %param.14) | copy-start | bytes 4128772
  6.0 7.5 %copy-start.9 = (f32[2,8]{1,0:T(2,128)S(1)}, f32[2,8]{1,0:T(2,128)}, u32[]{:S(2)}) copy-start(f32[2,8]{1,0:T(2,128)} %param.20) | copy-start | bytes 196
  6.0 40.4 %copy-start.4 = (bf16[256,768]{1,0:T(8,128)(2,1)S(1)}, bf16[256,768]{1,0:T(8,128)(2,1)}, u32[]{:S(2)}) copy-start(bf16[256,768]{1,0:T(8,128)(2,1)} %param.16) | copy-start | bytes 1179652
  7.2 39.2 %all-to-all-start = ((bf16[4,24,28,256]{3,1,2,0:T(8,128)(2,1)}), bf16[4,24,28,256]{3,1,2,0:T(8,128)(2,1)}, u32[]{:S(2)}, u32[]{:S(2)}) async-start(bf16[4,24,28,256]{3,1,2,0:T(8,128)(2,1)} %copy.106), calls=%async_computation | async-start | bytes 2752512 | tf_op jit(solution)/shard_map/all_to_all | solution.py:126
  101.0 0.9 copy-start.6
  139.0 1.1 copy-start.2
  141.8 21.7 %copy-start.5 = (bf16[256,768]{1,0:T(8,128)(2,1)S(1)}, bf16[256,768]{1,0:T(8,128)(2,1)}, u32[]{:S(2)}) copy-start(bf16[256,768]{1,0:T(8,128)(2,1)} %param.18) | copy-start | bytes 1179652
  141.8 21.6 %all-to-all-start.2 = ((bf16[96,4,7,256]{3,0,2,1:T(8,128)(2,1)}), bf16[96,4,7,256]{3,0,2,1:T(8,128)(2,1)S(1)}, u32[]{:S(2)}, u32[]{:S(2)}) async-start(bf16[96,4,7,256]{3,0,2,1:T(8,128)(2,1)} %bitcast.182), calls=%async_computation.2 | async-start | bytes 2752512 | tf_op jit(solution)/shard_map/all_to_all | solution.py:137
  234.6 2.2 copy-start.7
  261.2 1.3 copy-start.3
  262.6 4.3 %copy-start.8 = (f32[25,256]{1,0:T(8,128)S(1)}, f32[25,256]{1,0:T(8,128)}, u32[]{:S(2)}) copy-start(f32[25,256]{1,0:T(8,128)} %param.21) | copy-start | bytes 76804
  263.1 7.1 %collective-permute-start = (bf16[96,2,256]{2,0,1:T(8,128)(2,1)S(1)}, bf16[96,2,256]{2,0,1:T(8,128)(2,1)S(1)}, u32[]{:S(2)}, u32[]{:S(2)}) collective-permute-start(bf16[96,2,256]{2,0,1:T(8,128)(2,1)S(1)} %get-tuple-element.189), channel_id=1, source_target_pairs={{0,4},{4,8},{8,12},{12,0},{1,5},{5,9},{9,13},{13,1},{2,6},{6,10},{... | collective-permute-start | bytes 294920 | tf_op jit(solution)/shard_map/ppermute | solution.py:23
  263.5 6.6 %collective-permute-start.1 = (bf16[96,2,256]{2,0,1:T(8,128)(2,1)S(1)}, bf16[96,2,256]{2,0,1:T(8,128)(2,1)S(1)}, u32[]{:S(2)}, u32[]{:S(2)}) collective-permute-start(bf16[96,2,256]{2,0,1:T(8,128)(2,1)S(1)} %get-tuple-element.190), channel_id=1, source_target_pairs={{4,0},{8,4},{12,8},{0,12},{5,1},{9,5},{13,9},{1,13},{6,2},{10,6},{... | collective-permute-start | bytes 294920 | tf_op jit(solution)/shard_map/ppermute | solution.py:24
  270.2 2.8 collective-permute-start.2
  271.5 4.2 %collective-permute-start.3 = (bf16[2,32,256]{2,0,1:T(2,128)(2,1)S(1)}, bf16[2,32,256]{2,0,1:T(2,128)(2,1)S(1)}, u32[]{:S(2)}, u32[]{:S(2)}) collective-permute-start(bf16[2,32,256]{2,0,1:T(2,128)(2,1)S(1)} %get-tuple-element.188), channel_id=1, source_target_pairs={{1,0},{2,1},{3,2},{5,4},{6,5},{7,6},{9,8},{10,9},{11,10},{13,12},{... | collective-permute-start | bytes 98312 | tf_op jit(solution)/shard_map/ppermute | solution.py:24
  292.0 4.4 %copy-start.10 = (bf16[1024,256]{1,0:T(8,128)(2,1)S(1)}, bf16[1024,256]{1,0:T(8,128)(2,1)}, u32[]{:S(2)}) copy-start(bf16[1024,256]{1,0:T(8,128)(2,1)} %param.23) | copy-start | bytes 1572868
where the time goes:
time: 313 us; the launch traced here: 309 us
  matrix products  90.6 us (29%)
  blocking collectives  57.2 us (18%)
  waiting for transfers between devices  56.4 us (18%)
  local copies, waits for them, and re-layouts  44.8 us (14%)
  other arithmetic  42.3 us (14%)
  starting transfers between devices  16.9 us (5%)
    dot_general x16, matrix products, head_step(): jnp.einsum(EINSUM_FORMS[form][1], weights.astype(jnp.bfloat16), values_in...  41 us
    dot_general x16, matrix products, head_step(): jnp.einsum(EINSUM_FORMS[form][0], queries, keys_in, preferred_element_typ...  35.9 us
    all_to_all x1, blocking collectives, per_device(): lax.all_to_all(mixed_out.reshape(exchanged.shape), 'lon', split_axis=2, c...  34.7 us
    all_to_all x1, waiting for transfers between devices, per_device(): lax.all_to_all(stacked, 'lon', split_axis=0, concat_axis=2, tiled=True)  32.8 us
    all_to_all x1, blocking collectives, per_device(): lax.all_to_all(mixed_out.reshape(exchanged.shape), 'lat', split_axis=0, c...  22.5 us
    all_to_all x1, waiting for transfers between devices, per_device(): lax.all_to_all(stacked, 'lat', split_axis=1, concat_axis=0, tiled=True)  17.7 us
    reduce_sum x16, other arithmetic, head_step(): running_sum = running_sum * fading + jnp.sum(weights, -1)  12.5 us
    reduce_sum x3, other arithmetic, layer_norm(): average = jnp.mean(values, -1, keepdims=True)  11.1 us
  transfers between devices with their start and end apart: 6, of which 4 were waited for; matrix products, arithmetic and copies ran while one was open for 0% of the time, Pallas kernels for 0%

commit v1 on v0

v1 whole, which is shorter than its diff:
```python
import functools

import jax
import jax.numpy as jnp
from jax import lax
from jax.experimental import pallas as pl
from jax.experimental.pallas import tpu as pltpu
from jax.sharding import PartitionSpec as P

KERNEL = 5
MARGIN = KERNEL // 2
EPSILON = 1e-05
LOG2E = 1.4426950408889634
LANES = 128

NT = (((1,), (1,)), ((), ()))
TN = (((0,), (0,)), ((), ()))


def dot(a, b, dims=(((1,), (0,)), ((), ()))):
    return lax.dot_general(a, b, dims, preferred_element_type=jnp.float32)


def padded(n, unit):
    return -(-n // unit) * unit


def layer_norm(values, gains):
    average = jnp.mean(values, -1, keepdims=True)
    centred = values - average
    spread = jnp.mean(centred * centred, -1, keepdims=True)
    return centred * lax.rsqrt(spread + EPSILON) * gains


def attend_line(keys, queries_t, values_t, factors, diag, out_w, count, heads):
    size = queries_t.shape[0] // heads
    width = queries_t.shape[1]
    parts = []
    for h in range(heads):
        rows = slice(h * size, (h + 1) * size)
        diag[h, rows, :] = queries_t[rows]
        scores = dot(keys, diag[h])[:count]
        top = jnp.max(scores, 0, keepdims=True)
        weights = jnp.exp2((scores - top) * factors[h])
        total = jnp.sum(weights, 0, keepdims=True)
        rounded = weights.astype(jnp.bfloat16)
        if width > count:
            rounded = jnp.concatenate([rounded, jnp.zeros((width - count, width), jnp.bfloat16)], 0)
        parts.append((dot(values_t[rows], rounded) / total).astype(jnp.bfloat16))
    return dot(jnp.concatenate(parts, 0), out_w, TN)


def lon_kernel(factor_ref, x_ref, gain_ref, wk_ref, wqv_ref, wo_ref, o_ref, state, normed, diag, *, bands, blocks, count):
    cols, rows, features = x_ref.shape
    heads = diag.shape[0]
    width = diag.shape[2]
    diag[...] = jnp.zeros_like(diag)
    step = cols // bands
    lanes = [slice(c, c + LANES) for c in range(0, features, LANES)]

    @pl.loop(0, bands)
    def _(i):
        x = x_ref[pl.ds(i * step, step)].astype(jnp.float32).reshape(step * rows, features)
        y = layer_norm(x, gain_ref[...])
        at = pl.ds(pl.multiple_of(i * step * rows, 8), step * rows)
        for c, part in enumerate(lanes):
            state[c, at, :] = x[:, part]
            normed[c, at, :] = y[:, part]

    factors = [factor_ref[h] for h in range(heads)]

    @pl.loop(0, count)
    def _(r):
        at = pl.ds(r, cols, stride=rows)
        line = [normed.at[c][at, :].astype(jnp.bfloat16) for c in range(len(lanes))]
        line = jnp.concatenate(line, 1)
        if width > cols:
            line = jnp.concatenate([line, jnp.zeros((width - cols, features), jnp.bfloat16)], 0)
        keys = dot(line, wk_ref[...]).astype(jnp.bfloat16)
        both = dot(wqv_ref[...], line, NT).astype(jnp.bfloat16)
        mix = attend_line(keys, both[:features], both[features:], factors, diag, wo_ref[...], cols, heads)
        mix = mix[:cols].astype(jnp.bfloat16).astype(jnp.float32)
        for c, part in enumerate(lanes):
            state.at[c][at, :] = state.at[c][at, :] + mix[:, part]

    size = o_ref.shape[1]
    for i in range(bands):
        for j in range(blocks):
            at = slice((j * bands + i) * size * rows, (j * bands + i + 1) * size * rows)
            y = jnp.concatenate([state[c, at, :] for c in range(len(lanes))], 1)
            o_ref[i * blocks + j] = y.reshape(size, rows, features).astype(jnp.bfloat16)


def lat_kernel(factor_ref, x_ref, gain_ref, wk_ref, wqv_ref, wo_ref, o_ref, state, diag, *, bands):
    sources, _, rows, features = x_ref.shape
    length = sources * rows
    heads = diag.shape[0]

    @pl.when(pl.program_id(0) == 0)
    def _():
        diag[...] = jnp.zeros_like(diag)
        state[...] = jnp.zeros_like(state)

    x = x_ref[:, 0].astype(jnp.float32).reshape(length, features)
    line = layer_norm(x, gain_ref[...]).astype(jnp.bfloat16)
    keys = dot(line, wk_ref[...]).astype(jnp.bfloat16)
    both = dot(wqv_ref[...], line, NT).astype(jnp.bfloat16)
    factors = [factor_ref[h] for h in range(heads)]
    mix = attend_line(keys, both[:features], both[features:], factors, diag, wo_ref[...], length, heads)
    state[8 : 8 + length, :] = x + mix.astype(jnp.bfloat16).astype(jnp.float32)
    band = length // bands
    for i in range(bands):
        first = 8 + i * band - MARGIN
        o_ref[i, 0] = state[first : first + band + 2 * MARGIN, :].astype(jnp.bfloat16)


def mixer_kernel(s_ref, before_ref, after_ref, taps_ref, gain_ref, win_ref, wdown_ref, o_ref, wide, normed):
    cols, tall, features = s_ref.shape
    rows = tall - 2 * MARGIN
    step = o_ref.shape[0]
    hidden_len = wdown_ref.shape[0]
    g = pl.program_id(0)

    @pl.when(g == 0)
    def _():
        wide[:MARGIN, :tall] = before_ref[...].astype(jnp.float32)
        wide[MARGIN + cols :, :tall] = after_ref[...].astype(jnp.float32)
        wide[MARGIN : MARGIN + cols, :tall] = s_ref[...].astype(jnp.float32)

    for c in range(step):
        total = None
        for dy in range(KERNEL):
            part = None
            for dx in range(KERNEL):
                tap = taps_ref[dy * KERNEL + dx : dy * KERNEL + dx + 1, :]
                term = wide[g * step + c + dx, dy : dy + rows, :] * tap
                part = term if part is None else part + term
            total = part if total is None else total + part
        normed[c * rows : (c + 1) * rows, :] = layer_norm(total, gain_ref[...]).astype(jnp.bfloat16)

    for c in range(step):
        line = normed[c * rows : (c + 1) * rows, :]
        gate = dot(line, win_ref[:, :hidden_len])
        up = dot(line, win_ref[:, hidden_len:])
        hidden = (0.5 * gate * (1.0 + jnp.tanh(0.5 * gate)) * up).astype(jnp.bfloat16)
        update = dot(hidden, wdown_ref[...])
        kept = wide[g * step + c + MARGIN, MARGIN : MARGIN + rows, :]
        o_ref[c] = (kept + update).astype(jnp.bfloat16)


def whole(shape):
    return pl.BlockSpec(shape, lambda *_: (0,) * len(shape))


def split_weights(qkv, features):
    keys = qkv[:, features : 2 * features]
    both = jnp.concatenate([qkv[:, :features], qkv[:, 2 * features :]], 1).T
    return keys, both


def per_device(
    fields,
    norm_gains,
    lon_qkv,
    lon_out,
    lat_qkv,
    lat_out,
    logit_scales,
    conv_taps,
    mlp_in,
    mlp_down,
):
    lat_rows, lon_cols, features = fields.shape
    heads = logit_scales.shape[1]
    blocks = lax.axis_size("lon")
    bands = lax.axis_size("lat")
    sub_rows = lat_rows // blocks
    sub_cols = lon_cols // bands
    all_cols = lon_cols * blocks
    all_rows = lat_rows * bands
    factors = logit_scales * LOG2E
    smem = pl.BlockSpec(memory_space=pltpu.SMEM)
    bf16, f32 = jnp.bfloat16, jnp.float32

    stacked = jnp.transpose(fields.reshape(blocks, sub_rows, lon_cols, features), (0, 2, 1, 3))
    tall_rows = padded(sub_rows, 8)
    if tall_rows > sub_rows:
        stacked = jnp.pad(stacked, ((0, 0), (0, 0), (0, tall_rows - sub_rows), (0, 0)))
    lines = lax.all_to_all(stacked, "lon", split_axis=0, concat_axis=0, tiled=True)
    lines = lines.reshape(all_cols, tall_rows, features)
    wk, wqv = split_weights(lon_qkv, features)
    width = padded(all_cols, LANES)
    first_state = pl.pallas_call(
        functools.partial(lon_kernel, bands=bands, blocks=blocks, count=sub_rows),
        out_shape=jax.ShapeDtypeStruct((bands * blocks, sub_cols, tall_rows, features), bf16),
        in_specs=[smem] + [pl.BlockSpec(memory_space=pltpu.VMEM)] * 5,
        out_specs=pl.BlockSpec(memory_space=pltpu.VMEM),
        scratch_shapes=[
            pltpu.VMEM((features // LANES, all_cols * tall_rows, LANES), f32),
            pltpu.VMEM((features // LANES, all_cols * tall_rows, LANES), f32),
            pltpu.VMEM((heads, features, width), bf16),
        ],
        name="lon_attention",
    )(factors[0], lines, norm_gains[0:1], wk, wqv, lon_out)

    columns = lax.all_to_all(first_state, ("lat", "lon"), split_axis=0, concat_axis=0, tiled=True)
    if tall_rows > sub_rows:
        columns = jnp.swapaxes(columns[:, :, :sub_rows], 0, 1).reshape(1, sub_cols, all_rows, features)
    wk, wqv = split_weights(lat_qkv, features)
    tall = lat_rows + 2 * MARGIN
    second = pl.pallas_call(
        functools.partial(lat_kernel, bands=bands),
        grid=(sub_cols,),
        out_shape=jax.ShapeDtypeStruct((bands, sub_cols, tall, features), bf16),
        in_specs=[
            smem,
            pl.BlockSpec((columns.shape[0], 1, columns.shape[2], features), lambda k: (0, k, 0, 0)),
            whole((1, features)),
            whole((features, features)),
            whole((2 * features, features)),
            whole((features, features)),
        ],
        out_specs=pl.BlockSpec((bands, 1, tall, features), lambda k: (0, k, 0, 0)),
        scratch_shapes=[
            pltpu.VMEM((all_rows + 16, features), f32),
            pltpu.VMEM((heads, features, all_rows), bf16),
        ],
        name="lat_attention",
    )(factors[1], columns, norm_gains[1:2], wk, wqv, lat_out)

    block = lax.all_to_all(second, "lat", split_axis=0, concat_axis=0, tiled=True)
    block = block.reshape(lon_cols, tall, features)
    up = [(i, (i + 1) % blocks) for i in range(blocks)]
    before = lax.ppermute(block[lon_cols - MARGIN :], "lon", up)
    after = lax.ppermute(block[:MARGIN], "lon", [(j, i) for i, j in up])
    steps = bands
    mixed = pl.pallas_call(
        mixer_kernel,
        grid=(steps,),
        out_shape=jax.ShapeDtypeStruct((lon_cols, lat_rows, features), bf16),
        in_specs=[
            whole((lon_cols, tall, features)),
            whole((MARGIN, tall, features)),
            whole((MARGIN, tall, features)),
            whole(conv_taps.shape),
            whole((1, features)),
            whole(mlp_in.shape),
            whole(mlp_down.shape),
        ],
        out_specs=pl.BlockSpec((lon_cols // steps, lat_rows, features), lambda g: (g, 0, 0)),
        scratch_shapes=[
            pltpu.VMEM((lon_cols + 2 * MARGIN, padded(tall, 8), features), f32),
            pltpu.VMEM((lon_cols // steps * lat_rows, features), bf16),
        ],
        name="mixer",
    )(block, before, after, conv_taps, norm_gains[2:3], mlp_in, mlp_down)
    return jnp.transpose(mixed, (1, 0, 2))


def solution(mesh):
    in_specs = (P(("groups", "lat"), "lon", None), P(), P(), P(), P(), P(), P(), P(), P(), P())
    out_specs = P(("groups", "lat"), "lon", None)
    return jax.shard_map(
        per_device, mesh=mesh, in_specs=in_specs, out_specs=out_specs, check_vma=False
    )
```

time: 313 us -> 208 us (0.66); the launches traced: 309 us -> 208 us
  Pallas kernels: 0 us -> 95 us
  matrix products: 90.6 us -> 0 us
  other arithmetic: 42.3 us -> 1.44 us
  local copies, waits for them, and re-layouts: 44.8 us -> 8.32 us
  blocking collectives: 57.2 us -> 22.7 us
  waiting for transfers between devices: 56.4 us -> 66 us
    pallas_call x0 -> x3, Pallas kernels: none -> 95 us  [the longest x1 48.2 us: per_device(): pl.pallas_call(functools.partial(lon_kernel, bands=bands, blocks=blocks,...]
    dot_general x38 -> x0, matrix products: 90.6 us -> none  [the longest x16 41 us: head_step(): jnp.einsum(EINSUM_FORMS[form][1], weights.astype(jnp.bfloat16), values_in...]
    all_to_all x2 -> x1, blocking collectives: 57.2 us -> 22.7 us  [per_device(): lax.all_to_all(second, 'lat', split_axis=0, concat_axis=0, tiled=True)]
    reduce_sum x22 -> x0, other arithmetic: 27.7 us -> none  [the longest x16 12.5 us: head_step(): running_sum = running_sum * fading + jnp.sum(weights, -1)]
    slice x12 -> x4, local copies, waits for them, and re-layouts: 19.5 us -> 1.99 us  [the longest x2 1.38 us: split_weights(): both = jnp.concatenate([qkv[:, :features], qkv[:, 2 * features:]], 1).T]
    convert_element_type x10 -> x0, other arithmetic: 14.2 us -> none  [the longest x1 4.53 us: per_device(): return (second_state.astype(jnp.float32) + update).astype(jnp.bfloat16)]
    all_to_all x2, waiting for transfers between devices: 50.6 us -> 62.1 us  [the longest x1 32.2 us: per_device(): lax.all_to_all(first_state, ('lat', 'lon'), split_axis=0, concat_axis=0,...]
    dynamic_slice x16 -> x0, local copies, waits for them, and re-layouts: 9.85 us -> none  [attend_heads(): return lax.map(one_head, (state, queries, keys_in, values_in, factors))]
  transfers between devices with their start and end apart: 6 -> 4, of which waited for: 4 -> 3; matrix products, arithmetic and copies ran while one was open for 0% -> 2% of each run, Pallas kernels for 0% -> 0%
where the time goes in v1:
time: 208 us
  Pallas kernels  95 us (46%)
  waiting for transfers between devices  66 us (32%)
  blocking collectives  22.7 us (11%)
  starting transfers between devices  14.2 us (7%)
  local copies, waits for them, and re-layouts  8.32 us (4%)
    pallas_call x1, Pallas kernels, per_device(): pl.pallas_call(functools.partial(lon_kernel, bands=bands, blocks=blocks,...  48.2 us
    all_to_all x1, waiting for transfers between devices, per_device(): lax.all_to_all(first_state, ('lat', 'lon'), split_axis=0, concat_axis=0,...  32.2 us
    all_to_all x1, waiting for transfers between devices, per_device(): lax.all_to_all(stacked, 'lon', split_axis=0, concat_axis=0, tiled=True)  29.9 us
    pallas_call x1, Pallas kernels, per_device(): pl.pallas_call(functools.partial(lat_kernel, bands=bands), grid=(sub_cols...  28.9 us
    all_to_all x1, blocking collectives, per_device(): lax.all_to_all(second, 'lat', split_axis=0, concat_axis=0, tiled=True)  22.7 us
    pallas_call x1, Pallas kernels, per_device(): pl.pallas_call(mixer_kernel, grid=(steps,), out_shape=jax.ShapeDtypeStruc...  17.9 us
    all_to_all x1, starting transfers between devices, per_device(): lax.all_to_all(stacked, 'lon', split_axis=0, concat_axis=0, tiled=True)  6.48 us
  transfers between devices with their start and end apart: 4, of which 3 were waited for; matrix products, arithmetic and copies ran while one was open for 2% of the time, Pallas kernels for 0%

profile of v1, /device:TPU:0, one launch (start us, length us, event | category | flops | bytes accessed | tf_op | source)
XLA Modules:
  0.0 207.8 jit_solution(7725194006392183650)
XLA Ops:
  0.0 2.5 %copy.21 = bf16[4,24,28,256]{3,1,2,0:T(8,128)(2,1)} copy(bf16[4,24,28,256]{3,1,0,2:T(8,128)(2,1)} %bitcast.18) | data formatting | bytes 2752512 | tf_op jit(solution)/shard_map/reshape | solution.py:185
  2.5 6.5 %all-to-all-start = ((bf16[4,28,24,256]{3,2,1,0:T(8,128)(2,1)}), bf16[4,28,24,256]{3,2,1,0:T(8,128)(2,1)S(1)}, u32[]{:S(2)}, u32[]{:S(2)}) async-start(bf16[4,28,24,256]{3,2,1,0:T(8,128)(2,1)} %bitcast.14), calls=%async_computation | async-start | bytes 2752512 | tf_op jit(solution)/shard_map/all_to_all | solution.py:189
  9.0 0.0 copy-done.3
  9.0 0.7 fusion.2
  9.7 0.1 copy.16
  9.8 0.1 copy.17
  9.9 0.7 maximum_bitcast_fusion.wqv_ref
  10.6 0.0 copy-done.8
  10.6 0.6 slice_bitcast_fusion
  11.2 0.0 copy-done.7
  11.2 0.6 fusion.3
  11.8 29.9 %all-to-all-done = bf16[4,28,24,256]{3,2,1,0:T(8,128)(2,1)S(1)} async-done(((bf16[4,28,24,256]{3,2,1,0:T(8,128)(2,1)}), bf16[4,28,24,256]{3,2,1,0:T(8,128)(2,1)S(1)}, u32[]{:S(2)}, u32[]{:S(2)}) %all-to-all-start) | async-done | bytes 1376288 | tf_op jit(solution)/shard_map/all_to_all | solution.py:189
  41.7 1.1 copy-done.1
  42.8 48.2 %lon_attention.1 = bf16[16,7,24,256]{3,2,1,0:T(8,128)(2,1)} custom-call(f32[8]{0:T(128)} %get-tuple-element.16.factor_ref, bf16[112,24,256]{2,1,0:T(8,128)(2,1)} %bitcast.17, f32[1,256]{1,0:T(1,128)} %get-tuple-element.14.gain_ref, bf16[256,256]{1,0:T(8,128)(2,1)} %get-tuple-element.11.wk_ref, bf16[512,256]{1,0:T(8,128)(2,1)} %maximum_bitcast_fusion.wqv_ref, ...), custom_call_target="tpu_custom_call" | custom-call | tf_op jit(solution)/shard_map/lon_attention/pallas_call | solution.py:193
  91.0 3.9 %all-to-all-start.1 = ((bf16[16,7,24,256]{3,2,1,0:T(8,128)(2,1)}), bf16[16,7,24,256]{3,2,1,0:T(8,128)(2,1)S(1)}, u32[]{:S(2)}, u32[]{:S(2)}) async-start(bf16[16,7,24,256]{3,2,1,0:T(8,128)(2,1)} %lon_attention.1), calls=%async_computation.1 | async-start | bytes 2752512 | tf_op jit(solution)/shard_map/all_to_all | solution.py:206
  94.9 0.0 copy-done.4
  95.0 0.7 fusion.1
  95.7 0.1 copy.18
  95.8 0.1 copy.19
  95.9 0.7 maximum_bitcast_fusion.1.wqv_ref
  96.6 32.2 %all-to-all-done.1.x_ref = bf16[16,7,24,256]{3,2,1,0:T(8,128)(2,1)S(1)} async-done(((bf16[16,7,24,256]{3,2,1,0:T(8,128)(2,1)}), bf16[16,7,24,256]{3,2,1,0:T(8,128)(2,1)S(1)}, u32[]{:S(2)}, u32[]{:S(2)}) %all-to-all-start.1) | async-done | bytes 1376288 | tf_op jit(solution)/shard_map/all_to_all | solution.py:206
  128.8 1.1 copy-done.2
  129.9 28.9 %lat_attention.1 = bf16[4,7,100,256]{3,2,1,0:T(8,128)(2,1)} custom-call(f32[8]{0:T(128)} %get-tuple-element.17.factor_ref, bf16[16,7,24,256]{3,2,1,0:T(8,128)(2,1)} %copy-done.2, f32[1,256]{1,0:T(1,128)} %get-tuple-element.15.gain_ref, bf16[256,256]{1,0:T(8,128)(2,1)} %get-tuple-element.8.wk_ref, bf16[512,256]{1,0:T(8,128)(2,1)} %maximum_bitcast_fusion.1.wqv_ref, ...), custom_call_target="tpu_custom_call" | custom-call | tf_op jit(solution)/shard_map/lat_attention/pallas_call | solution.py:211
  158.8 22.7 %all_to_all.15 = bf16[4,7,100,256]{3,2,1,0:T(8,128)(2,1)S(1)} all-to-all(bf16[4,7,100,256]{3,2,1,0:T(8,128)(2,1)} %lat_attention.1), channel_id=1, replica_groups=mesh['groups'=2,'lon'=4,'lat'=4] {'lat'}, dimensions={0} | all-to-all | bytes 2867200 | tf_op jit(solution)/shard_map/all_to_all | solution.py:231
  181.5 0.1 collective-permute-start
  181.6 3.8 %collective-permute-start.1 = (bf16[2,100,256]{2,1,0:T(8,128)(2,1)S(1)}, bf16[2,100,256]{2,1,0:T(8,128)(2,1)S(1)}, u32[]{:S(2)}, u32[]{:S(2)}) collective-permute-start(bf16[2,100,256]{2,1,0:T(8,128)(2,1)S(1)} %get-tuple-element.5), channel_id=1, source_target_pairs={{4,0},{8,4},{12,8},{0,12},{5,1},{9,5},{13,9},{1,13},{6,2},{10,6},{... | collective-permute-start | bytes 307208 | tf_op jit(solution)/shard_map/ppermute | solution.py:235
  185.4 3.8 %collective-permute-done.before_ref = bf16[2,100,256]{2,1,0:T(8,128)(2,1)S(1)} collective-permute-done((bf16[2,100,256]{2,1,0:T(8,128)(2,1)S(1)}, bf16[2,100,256]{2,1,0:T(8,128)(2,1)S(1)}, u32[]{:S(2)}, u32[]{:S(2)}) %collective-permute-start) | collective-permute-done | bytes 102432 | tf_op jit(solution)/shard_map/ppermute | solution.py:234
  189.2 0.0 collective-permute-done.1.after_ref
  189.2 0.0 copy-done
  189.2 0.6 copy-done.5
  189.9 0.1 copy-done.6
  189.9 17.9 %mixer.1 = bf16[28,96,256]{2,1,0:T(8,128)(2,1)} custom-call(bf16[28,100,256]{2,1,0:T(8,128)(2,1)} %bitcast.16, bf16[2,100,256]{2,1,0:T(8,128)(2,1)} %copy-done.5, bf16[2,100,256]{2,1,0:T(8,128)(2,1)} %copy-done.6, f32[25,256]{1,0:T(8,128)} %taps_ref.1, f32[1,256]{1,0:T(1,128)} %get-tuple-element.13.gain_ref, bf16[256,2048]{1,0:T(8,128)(2,1)} %win_ref.1, ...), custom_call_target="tpu_custom_call" | custom-call | tf_op jit(solution)/shard_map/mixer/pallas_call | solution.py:237
  (11 shorter events, 0.0 us)
Async XLA Ops:
  2.5 6.5 %copy-start.3 = (bf16[256,768]{1,0:T(8,128)(2,1)S(1)}, bf16[256,768]{1,0:T(8,128)(2,1)}, u32[]{:S(2)}) copy-start(bf16[256,768]{1,0:T(8,128)(2,1)} %param.12) | copy-start | bytes 1179652
  2.5 39.2 %all-to-all-start = ((bf16[4,28,24,256]{3,2,1,0:T(8,128)(2,1)}), bf16[4,28,24,256]{3,2,1,0:T(8,128)(2,1)S(1)}, u32[]{:S(2)}, u32[]{:S(2)}) async-start(bf16[4,28,24,256]{3,2,1,0:T(8,128)(2,1)} %bitcast.14), calls=%async_computation | async-start | bytes 2752512 | tf_op jit(solution)/shard_map/all_to_all | solution.py:189
  9.0 1.6 copy-start.8
  9.0 2.2 %copy-start.7 = (f32[3,256]{1,0:T(4,128)S(1)}, f32[3,256]{1,0:T(4,128)}, u32[]{:S(2)}) copy-start(f32[3,256]{1,0:T(4,128)} %param.11) | copy-start | bytes 9220
  41.7 1.1 copy-start.1
  91.0 3.9 %copy-start.4 = (bf16[256,768]{1,0:T(8,128)(2,1)S(1)}, bf16[256,768]{1,0:T(8,128)(2,1)}, u32[]{:S(2)}) copy-start(bf16[256,768]{1,0:T(8,128)(2,1)} %param.14) | copy-start | bytes 1179652
  91.0 37.8 %all-to-all-start.1 = ((bf16[16,7,24,256]{3,2,1,0:T(8,128)(2,1)}), bf16[16,7,24,256]{3,2,1,0:T(8,128)(2,1)S(1)}, u32[]{:S(2)}, u32[]{:S(2)}) async-start(bf16[16,7,24,256]{3,2,1,0:T(8,128)(2,1)} %lon_attention.1), calls=%async_computation.1 | async-start | bytes 2752512 | tf_op jit(solution)/shard_map/all_to_all | solution.py:206
  128.8 1.1 copy-start.2
  181.5 7.7 %copy-start = (bf16[4,7,100,256]{3,2,1,0:T(8,128)(2,1)}, bf16[4,7,100,256]{3,2,1,0:T(8,128)(2,1)S(1)}, u32[]{:S(2)}) copy-start(bf16[4,7,100,256]{3,2,1,0:T(8,128)(2,1)S(1)} %all_to_all.15) | copy-start | bytes 4300804
  181.5 7.7 %collective-permute-start = (bf16[2,100,256]{2,1,0:T(8,128)(2,1)S(1)}, bf16[2,100,256]{2,1,0:T(8,128)(2,1)S(1)}, u32[]{:S(2)}, u32[]{:S(2)}) collective-permute-start(bf16[2,100,256]{2,1,0:T(8,128)(2,1)S(1)} %get-tuple-element.6), channel_id=1, source_target_pairs={{0,4},{4,8},{8,12},{12,0},{1,5},{5,9},{9,13},{13,1},{2,6},{6,10},{... | collective-permute-start | bytes 307208 | tf_op jit(solution)/shard_map/ppermute | solution.py:234
  181.6 7.6 %collective-permute-start.1 = (bf16[2,100,256]{2,1,0:T(8,128)(2,1)S(1)}, bf16[2,100,256]{2,1,0:T(8,128)(2,1)S(1)}, u32[]{:S(2)}, u32[]{:S(2)}) collective-permute-start(bf16[2,100,256]{2,1,0:T(8,128)(2,1)S(1)} %get-tuple-element.5), channel_id=1, source_target_pairs={{4,0},{8,4},{12,8},{0,12},{5,1},{9,5},{13,9},{1,13},{6,2},{10,6},{... | collective-permute-start | bytes 307208 | tf_op jit(solution)/shard_map/ppermute | solution.py:235
  189.2 0.6 copy-start.5
  189.2 0.7 copy-start.6

commit v2 on v1

v2 whole, which is shorter than its diff:
```python
import functools

import jax
import jax.numpy as jnp
from jax import lax
from jax.experimental import pallas as pl
from jax.experimental.pallas import tpu as pltpu
from jax.sharding import PartitionSpec as P

KERNEL = 5
MARGIN = KERNEL // 2
EPSILON = 1e-05
LOG2E = 1.4426950408889634
LANES = 128

NT = (((1,), (1,)), ((), ()))
TN = (((0,), (0,)), ((), ()))


def dot(a, b, dims=(((1,), (0,)), ((), ()))):
    return lax.dot_general(a, b, dims, preferred_element_type=jnp.float32)


def padded(n, unit):
    return -(-n // unit) * unit


def layer_norm(values, gains):
    average = jnp.mean(values, -1, keepdims=True)
    centred = values - average
    spread = jnp.mean(centred * centred, -1, keepdims=True)
    return centred * lax.rsqrt(spread + EPSILON) * gains


def attend_line(keys, both, factors, diag, out_w, group):
    features = keys.shape[1]
    heads = len(factors)
    size = features // heads
    parts = [None] * heads
    for h in range(heads):
        rows = slice(h * size, (h + 1) * size)
        diag[h, rows, :] = both[rows]
    for start in range(0, heads, group):
        some = range(start, start + group)
        scores = {h: dot(keys, diag[h]) for h in some}
        rounded, total = {}, {}
        for h in some:
            top = jnp.max(scores[h], 0, keepdims=True)
            weights = jnp.exp2((scores[h] - top) * factors[h])
            total[h] = jnp.sum(weights, 0, keepdims=True)
            rounded[h] = weights.astype(jnp.bfloat16)
        for h in some:
            values = both[features + h * size : features + (h + 1) * size]
            parts[h] = (dot(values, rounded[h]) / total[h]).astype(jnp.bfloat16)
    return dot(jnp.concatenate(parts, 0), out_w, TN)


def attend_lines(keys, both, factors, diag, out_w, count, width, heads, lines):
    features = keys.shape[1]
    size = features // heads
    pairs = [(u, h) for u in range(lines) for h in range(heads)]
    parts = {}
    scores = {}
    for u, h in pairs:
        rows = slice(h * size, (h + 1) * size)
        diag[u * heads + h, rows, :] = both[rows, u * width : (u + 1) * width]
    for u, h in pairs:
        scores[u, h] = dot(keys[u * width : u * width + count], diag[u * heads + h])
    rounded, total = {}, {}
    for u, h in pairs:
        top = jnp.max(scores[u, h], 0, keepdims=True)
        weights = jnp.exp2((scores[u, h] - top) * factors[h])
        total[u, h] = jnp.sum(weights, 0, keepdims=True)
        packed = weights.astype(jnp.bfloat16)
        if width > count:
            packed = jnp.concatenate([packed, jnp.zeros((width - count, width), jnp.bfloat16)], 0)
        rounded[u, h] = packed
    for u, h in pairs:
        values = both[features + h * size : features + (h + 1) * size, u * width : (u + 1) * width]
        parts[u, h] = (dot(values, rounded[u, h]) / total[u, h]).astype(jnp.bfloat16)
    context = [jnp.concatenate([parts[u, h] for h in range(heads)], 0) for u in range(lines)]
    return dot(jnp.concatenate(context, 1), out_w, TN)


def lon_kernel(factor_ref, x_ref, gain_ref, wk_ref, wqv_ref, wo_ref, o_ref, state, normed, diag, *, bands, blocks, count):
    cols, rows, features = x_ref.shape
    heads = factor_ref.shape[0]
    width = diag.shape[2]
    diag[...] = jnp.zeros_like(diag)
    step = cols // bands
    lanes = [slice(c, c + LANES) for c in range(0, features, LANES)]

    @pl.loop(0, bands)
    def _(i):
        x = x_ref[pl.ds(i * step, step)].astype(jnp.float32).reshape(step * rows, features)
        y = layer_norm(x, gain_ref[...])
        at = pl.ds(pl.multiple_of(i * step * rows, 8), step * rows)
        for c, part in enumerate(lanes):
            state[c, at, :] = x[:, part]
            normed[c, at, :] = y[:, part]

    factors = [factor_ref[h] for h in range(heads)]

    unroll = diag.shape[0] // heads

    @pl.loop(0, count // unroll)
    def _(group):
        spots = [pl.ds(group * unroll + u, cols, stride=rows) for u in range(unroll)]
        lines = []
        for at in spots:
            line = [normed.at[c][at, :].astype(jnp.bfloat16) for c in range(len(lanes))]
            line = jnp.concatenate(line, 1)
            if width > cols:
                line = jnp.concatenate([line, jnp.zeros((width - cols, features), jnp.bfloat16)], 0)
            lines.append(line)
        stack = jnp.concatenate(lines, 0)
        keys = dot(stack, wk_ref[...]).astype(jnp.bfloat16)
        both = dot(wqv_ref[...], stack, NT).astype(jnp.bfloat16)
        mixes = attend_lines(keys, both, factors, diag, wo_ref[...], cols, width, heads, unroll)
        for u, at in enumerate(spots):
            mix = mixes[u * width : u * width + cols].astype(jnp.bfloat16).astype(jnp.float32)
            for c, part in enumerate(lanes):
                state.at[c][at, :] = state.at[c][at, :] + mix[:, part]

    size = o_ref.shape[1]
    for i in range(bands):
        for j in range(blocks):
            at = slice((j * bands + i) * size * rows, (j * bands + i + 1) * size * rows)
            y = jnp.concatenate([state[c, at, :] for c in range(len(lanes))], 1)
            o_ref[i * blocks + j] = y.reshape(size, rows, features).astype(jnp.bfloat16)


def lat_kernel(factor_ref, x_ref, gain_ref, wk_ref, wqv_ref, wo_ref, o_ref, state, diag, *, bands):
    sources, _, rows, features = x_ref.shape
    length = sources * rows
    heads = diag.shape[0]

    @pl.when(pl.program_id(0) == 0)
    def _():
        diag[...] = jnp.zeros_like(diag)
        state[...] = jnp.zeros_like(state)

    x = x_ref[:, 0].astype(jnp.float32).reshape(length, features)
    line = layer_norm(x, gain_ref[...]).astype(jnp.bfloat16)
    keys = dot(line, wk_ref[...]).astype(jnp.bfloat16)
    both = dot(wqv_ref[...], line, NT).astype(jnp.bfloat16)
    factors = [factor_ref[h] for h in range(heads)]
    mix = attend_line(keys, both, factors, diag, wo_ref[...], 8)
    state[8 : 8 + length, :] = x + mix.astype(jnp.bfloat16).astype(jnp.float32)
    band = length // bands
    for i in range(bands):
        first = 8 + i * band - MARGIN
        o_ref[i, 0] = state[first : first + band + 2 * MARGIN, :].astype(jnp.bfloat16)


def mixer_kernel(s_ref, before_ref, after_ref, taps_ref, gain_ref, win_ref, wdown_ref, o_ref, wide, normed):
    cols, tall, features = s_ref.shape
    rows = tall - 2 * MARGIN
    step = o_ref.shape[0]
    hidden_len = wdown_ref.shape[0]
    g = pl.program_id(0)

    @pl.when(g == 0)
    def _():
        wide[:MARGIN, :tall] = before_ref[...].astype(jnp.float32)
        wide[MARGIN + cols :, :tall] = after_ref[...].astype(jnp.float32)
        wide[MARGIN : MARGIN + cols, :tall] = s_ref[...].astype(jnp.float32)

    for c in range(step):
        total = None
        for dy in range(KERNEL):
            part = None
            for dx in range(KERNEL):
                tap = taps_ref[dy * KERNEL + dx : dy * KERNEL + dx + 1, :]
                term = wide[g * step + c + dx, dy : dy + rows, :] * tap
                part = term if part is None else part + term
            total = part if total is None else total + part
        normed[c * rows : (c + 1) * rows, :] = layer_norm(total, gain_ref[...]).astype(jnp.bfloat16)

    for c in range(step):
        line = normed[c * rows : (c + 1) * rows, :]
        gate = dot(line, win_ref[:, :hidden_len])
        up = dot(line, win_ref[:, hidden_len:])
        hidden = (0.5 * gate * (1.0 + jnp.tanh(0.5 * gate)) * up).astype(jnp.bfloat16)
        update = dot(hidden, wdown_ref[...])
        kept = wide[g * step + c + MARGIN, MARGIN : MARGIN + rows, :]
        o_ref[c] = (kept + update).astype(jnp.bfloat16)


def whole(shape):
    return pl.BlockSpec(shape, lambda *_: (0,) * len(shape))


def split_weights(qkv, features):
    keys = qkv[:, features : 2 * features]
    both = jnp.concatenate([qkv[:, :features], qkv[:, 2 * features :]], 1).T
    return keys, both


SMEM = pl.BlockSpec(memory_space=pltpu.SMEM)
VMEM = pl.BlockSpec(memory_space=pltpu.VMEM)


def lon_call(lines, factors, gains, qkv, out_w, bands, blocks, count):
    all_cols, rows, features = lines.shape
    heads = factors.shape[0]
    wk, wqv = split_weights(qkv, features)
    unroll = next(u for u in (8, 2, 1) if u == 1 or (count % u == 0 and all_cols <= 2 * LANES))
    return pl.pallas_call(
        functools.partial(lon_kernel, bands=bands, blocks=blocks, count=count),
        out_shape=jax.ShapeDtypeStruct(
            (bands * blocks, all_cols // (bands * blocks), rows, features), jnp.bfloat16
        ),
        in_specs=[SMEM] + [VMEM] * 5,
        out_specs=VMEM,
        scratch_shapes=[
            pltpu.VMEM((features // LANES, all_cols * rows, LANES), jnp.float32),
            pltpu.VMEM((features // LANES, all_cols * rows, LANES), jnp.float32),
            pltpu.VMEM((heads * unroll, features, padded(all_cols, LANES)), jnp.bfloat16),
        ],
        name="lon_attention",
    )(factors, lines, gains, wk, wqv, out_w)


def lat_call(columns, factors, gains, qkv, out_w, bands):
    sources, count, rows, features = columns.shape
    heads = factors.shape[0]
    length = sources * rows
    tall = length // bands + 2 * MARGIN
    wk, wqv = split_weights(qkv, features)
    return pl.pallas_call(
        functools.partial(lat_kernel, bands=bands),
        grid=(count,),
        out_shape=jax.ShapeDtypeStruct((bands, count, tall, features), jnp.bfloat16),
        in_specs=[
            SMEM,
            pl.BlockSpec((sources, 1, rows, features), lambda k: (0, k, 0, 0)),
            whole((1, features)),
            whole((features, features)),
            whole((2 * features, features)),
            whole((features, features)),
        ],
        out_specs=pl.BlockSpec((bands, 1, tall, features), lambda k: (0, k, 0, 0)),
        scratch_shapes=[
            pltpu.VMEM((length + 16, features), jnp.float32),
            pltpu.VMEM((heads, features, length), jnp.bfloat16),
        ],
        name="lat_attention",
    )(factors, columns, gains, wk, wqv, out_w)


def mixer_call(block, before, after, taps, gains, win, wdown, steps):
    cols, tall, features = block.shape
    rows = tall - 2 * MARGIN
    return pl.pallas_call(
        mixer_kernel,
        grid=(steps,),
        out_shape=jax.ShapeDtypeStruct((cols, rows, features), jnp.bfloat16),
        in_specs=[
            whole(block.shape),
            whole(before.shape),
            whole(after.shape),
            whole(taps.shape),
            whole(gains.shape),
            whole(win.shape),
            whole(wdown.shape),
        ],
        out_specs=pl.BlockSpec((cols // steps, rows, features), lambda g: (g, 0, 0)),
        scratch_shapes=[
            pltpu.VMEM((cols + 2 * MARGIN, padded(tall, 8), features), jnp.float32),
            pltpu.VMEM((cols // steps * rows, features), jnp.bfloat16),
        ],
        name="mixer",
    )(block, before, after, taps, gains, win, wdown)


def per_device(
    fields,
    norm_gains,
    lon_qkv,
    lon_out,
    lat_qkv,
    lat_out,
    logit_scales,
    conv_taps,
    mlp_in,
    mlp_down,
):
    lat_rows, lon_cols, features = fields.shape
    blocks = lax.axis_size("lon")
    bands = lax.axis_size("lat")
    sub_rows = lat_rows // blocks
    tall_rows = padded(sub_rows, 8)
    sub_cols = lon_cols // bands
    all_cols = lon_cols * blocks
    all_rows = lat_rows * bands
    tall = lat_rows + 2 * MARGIN
    factors = logit_scales * LOG2E

    stacked = jnp.transpose(fields.reshape(blocks, sub_rows, lon_cols, features), (0, 2, 1, 3))
    if tall_rows > sub_rows:
        stacked = jnp.pad(stacked, ((0, 0), (0, 0), (0, tall_rows - sub_rows), (0, 0)))
    lines = lax.all_to_all(stacked, "lon", split_axis=0, concat_axis=0, tiled=True)
    lines = lines.reshape(all_cols, tall_rows, features)
    first_state = lon_call(
        lines, factors[0], norm_gains[0:1], lon_qkv, lon_out, bands, blocks, sub_rows
    )

    columns = lax.all_to_all(first_state, ("lat", "lon"), split_axis=0, concat_axis=0, tiled=True)
    if tall_rows > sub_rows:
        columns = jnp.swapaxes(columns[:, :, :sub_rows], 0, 1).reshape(1, sub_cols, all_rows, features)
    second = lat_call(columns, factors[1], norm_gains[1:2], lat_qkv, lat_out, bands)

    block = lax.all_to_all(second, "lat", split_axis=0, concat_axis=0, tiled=True)
    block = block.reshape(lon_cols, tall, features)
    up = [(i, (i + 1) % blocks) for i in range(blocks)]
    before = lax.ppermute(block[lon_cols - MARGIN :], "lon", up)
    after = lax.ppermute(block[:MARGIN], "lon", [(j, i) for i, j in up])
    mixed = mixer_call(block, before, after, conv_taps, norm_gains[2:3], mlp_in, mlp_down, bands)
    return jnp.transpose(mixed, (1, 0, 2))


def solution(mesh):
    in_specs = (P(("groups", "lat"), "lon", None), P(), P(), P(), P(), P(), P(), P(), P(), P())
    out_specs = P(("groups", "lat"), "lon", None)
    return jax.shard_map(
        per_device, mesh=mesh, in_specs=in_specs, out_specs=out_specs, check_vma=False
    )
```

time: 208 us -> 161 us (0.77)
  Pallas kernels: 95 us -> 48.1 us
    pallas_call x3, Pallas kernels: 95 us -> 48.1 us  [the longest x1 18.7 us: lat_call(): pl.pallas_call(functools.partial(lat_kernel, bands=bands), grid=(count,),...]
  transfers between devices with their start and end apart: 4 -> 4, of which waited for: 3 -> 3; matrix products, arithmetic and copies ran while one was open for 2% -> 3% of each run, Pallas kernels for 0% -> 0%
where the time goes in v2:
time: 161 us
  waiting for transfers between devices  66 us (41%)
  Pallas kernels  48.1 us (30%)
  blocking collectives  22.7 us (14%)
  starting transfers between devices  14.2 us (9%)
  local copies, waits for them, and re-layouts  8.32 us (5%)
    all_to_all x1, waiting for transfers between devices, per_device(): lax.all_to_all(first_state, ('lat', 'lon'), split_axis=0, concat_axis=0,...  32.2 us
    all_to_all x1, waiting for transfers between devices, per_device(): lax.all_to_all(stacked, 'lon', split_axis=0, concat_axis=0, tiled=True)  29.9 us
    all_to_all x1, blocking collectives, per_device(): lax.all_to_all(second, 'lat', split_axis=0, concat_axis=0, tiled=True)  22.7 us
    pallas_call x1, Pallas kernels, lat_call(): pl.pallas_call(functools.partial(lat_kernel, bands=bands), grid=(count,),...  18.7 us
    pallas_call x1, Pallas kernels, mixer_call(): pl.pallas_call(mixer_kernel, grid=(steps,), out_shape=jax.ShapeDtypeStruc...  17.9 us
    pallas_call x1, Pallas kernels, lon_call(): pl.pallas_call(functools.partial(lon_kernel, bands=bands, blocks=blocks,...  11.5 us
    all_to_all x1, starting transfers between devices, per_device(): lax.all_to_all(stacked, 'lon', split_axis=0, concat_axis=0, tiled=True)  6.48 us
    all_to_all x1, starting transfers between devices, per_device(): lax.all_to_all(first_state, ('lat', 'lon'), split_axis=0, concat_axis=0,...  3.9 us
  transfers between devices with their start and end apart: 4, of which 3 were waited for; matrix products, arithmetic and copies ran while one was open for 3% of the time, Pallas kernels for 0%

profile of v2, /device:TPU:0, one launch (start us, length us, event | category | flops | bytes accessed | tf_op | source)
XLA Modules:
  0.0 160.8 jit_solution(12927161949281487912)
XLA Ops:
  0.0 2.5 %copy.21 = bf16[4,24,28,256]{3,1,2,0:T(8,128)(2,1)} copy(bf16[4,24,28,256]{3,1,0,2:T(8,128)(2,1)} %bitcast.18) | data formatting | bytes 2752512 | tf_op jit(solution)/shard_map/reshape | solution.py:300
  2.5 6.5 %all-to-all-start = ((bf16[4,28,24,256]{3,2,1,0:T(8,128)(2,1)}), bf16[4,28,24,256]{3,2,1,0:T(8,128)(2,1)S(1)}, u32[]{:S(2)}, u32[]{:S(2)}) async-start(bf16[4,28,24,256]{3,2,1,0:T(8,128)(2,1)} %bitcast.14), calls=%async_computation | async-start | bytes 2752512 | tf_op jit(solution)/shard_map/all_to_all | solution.py:303
  9.0 0.0 copy-done.3
  9.0 0.7 fusion.2
  9.7 0.1 copy.16
  9.8 0.1 copy.17
  9.9 0.7 maximum_bitcast_fusion.wqv_ref
  10.6 0.0 copy-done.8
  10.6 0.6 slice_bitcast_fusion
  11.2 0.0 copy-done.7
  11.2 0.6 fusion.3
  11.8 29.9 %all-to-all-done = bf16[4,28,24,256]{3,2,1,0:T(8,128)(2,1)S(1)} async-done(((bf16[4,28,24,256]{3,2,1,0:T(8,128)(2,1)}), bf16[4,28,24,256]{3,2,1,0:T(8,128)(2,1)S(1)}, u32[]{:S(2)}, u32[]{:S(2)}) %all-to-all-start) | async-done | bytes 1376288 | tf_op jit(solution)/shard_map/all_to_all | solution.py:303
  41.7 1.1 copy-done.1
  42.8 11.5 %lon_attention.1 = bf16[16,7,24,256]{3,2,1,0:T(8,128)(2,1)} custom-call(f32[8]{0:T(128)} %get-tuple-element.16.factor_ref, bf16[112,24,256]{2,1,0:T(8,128)(2,1)} %bitcast.17, f32[1,256]{1,0:T(1,128)} %get-tuple-element.14.gain_ref, bf16[256,256]{1,0:T(8,128)(2,1)} %get-tuple-element.11.wk_ref, bf16[512,256]{1,0:T(8,128)(2,1)} %maximum_bitcast_fusion.wqv_ref, ...), custom_call_target="tpu_custom_call" | custom-call | tf_op jit(solution)/shard_map/lon_attention/pallas_call | solution.py:209
  54.3 3.9 %all-to-all-start.1 = ((bf16[16,7,24,256]{3,2,1,0:T(8,128)(2,1)}), bf16[16,7,24,256]{3,2,1,0:T(8,128)(2,1)S(1)}, u32[]{:S(2)}, u32[]{:S(2)}) async-start(bf16[16,7,24,256]{3,2,1,0:T(8,128)(2,1)} %lon_attention.1), calls=%async_computation.1 | async-start | bytes 2752512 | tf_op jit(solution)/shard_map/all_to_all | solution.py:309
  58.2 0.0 copy-done.4
  58.2 0.7 fusion.1
  58.9 0.1 copy.18
  59.0 0.1 copy.19
  59.1 0.7 maximum_bitcast_fusion.1.wqv_ref
  59.9 32.2 %all-to-all-done.1.x_ref = bf16[16,7,24,256]{3,2,1,0:T(8,128)(2,1)S(1)} async-done(((bf16[16,7,24,256]{3,2,1,0:T(8,128)(2,1)}), bf16[16,7,24,256]{3,2,1,0:T(8,128)(2,1)S(1)}, u32[]{:S(2)}, u32[]{:S(2)}) %all-to-all-start.1) | async-done | bytes 1376288 | tf_op jit(solution)/shard_map/all_to_all | solution.py:309
  92.1 1.1 copy-done.2
  93.2 18.7 %lat_attention.1 = bf16[4,7,100,256]{3,2,1,0:T(8,128)(2,1)} custom-call(f32[8]{0:T(128)} %get-tuple-element.17.factor_ref, bf16[16,7,24,256]{3,2,1,0:T(8,128)(2,1)} %copy-done.2, f32[1,256]{1,0:T(1,128)} %get-tuple-element.15.gain_ref, bf16[256,256]{1,0:T(8,128)(2,1)} %get-tuple-element.8.wk_ref, bf16[512,256]{1,0:T(8,128)(2,1)} %maximum_bitcast_fusion.1.wqv_ref, ...), custom_call_target="tpu_custom_call" | custom-call | tf_op jit(solution)/shard_map/lat_attention/pallas_call | solution.py:231
  111.9 22.7 %all_to_all.15 = bf16[4,7,100,256]{3,2,1,0:T(8,128)(2,1)S(1)} all-to-all(bf16[4,7,100,256]{3,2,1,0:T(8,128)(2,1)} %lat_attention.1), channel_id=1, replica_groups=mesh['groups'=2,'lon'=4,'lat'=4] {'lat'}, dimensions={0} | all-to-all | bytes 2867200 | tf_op jit(solution)/shard_map/all_to_all | solution.py:314
  134.6 0.1 collective-permute-start
  134.6 3.8 %collective-permute-start.1 = (bf16[2,100,256]{2,1,0:T(8,128)(2,1)S(1)}, bf16[2,100,256]{2,1,0:T(8,128)(2,1)S(1)}, u32[]{:S(2)}, u32[]{:S(2)}) collective-permute-start(bf16[2,100,256]{2,1,0:T(8,128)(2,1)S(1)} %get-tuple-element.5), channel_id=1, source_target_pairs={{4,0},{8,4},{12,8},{0,12},{5,1},{9,5},{13,9},{1,13},{6,2},{10,6},{... | collective-permute-start | bytes 307208 | tf_op jit(solution)/shard_map/ppermute | solution.py:318
  138.5 3.8 %collective-permute-done.before_ref = bf16[2,100,256]{2,1,0:T(8,128)(2,1)S(1)} collective-permute-done((bf16[2,100,256]{2,1,0:T(8,128)(2,1)S(1)}, bf16[2,100,256]{2,1,0:T(8,128)(2,1)S(1)}, u32[]{:S(2)}, u32[]{:S(2)}) %collective-permute-start) | collective-permute-done | bytes 102432 | tf_op jit(solution)/shard_map/ppermute | solution.py:317
  142.3 0.0 collective-permute-done.1.after_ref
  142.3 0.0 copy-done
  142.3 0.6 copy-done.5
  142.9 0.1 copy-done.6
  143.0 17.9 %mixer.1 = bf16[28,96,256]{2,1,0:T(8,128)(2,1)} custom-call(bf16[28,100,256]{2,1,0:T(8,128)(2,1)} %bitcast.16, bf16[2,100,256]{2,1,0:T(8,128)(2,1)} %copy-done.5, bf16[2,100,256]{2,1,0:T(8,128)(2,1)} %copy-done.6, f32[25,256]{1,0:T(8,128)} %taps_ref.1, f32[1,256]{1,0:T(1,128)} %get-tuple-element.13.gain_ref, bf16[256,2048]{1,0:T(8,128)(2,1)} %win_ref.1, ...), custom_call_target="tpu_custom_call" | custom-call | tf_op jit(solution)/shard_map/mixer/pallas_call | solution.py:255
  (11 shorter events, 0.0 us)
Async XLA Ops:
  2.5 6.5 %copy-start.3 = (bf16[256,768]{1,0:T(8,128)(2,1)S(1)}, bf16[256,768]{1,0:T(8,128)(2,1)}, u32[]{:S(2)}) copy-start(bf16[256,768]{1,0:T(8,128)(2,1)} %param.12) | copy-start | bytes 1179652
  2.5 39.2 %all-to-all-start = ((bf16[4,28,24,256]{3,2,1,0:T(8,128)(2,1)}), bf16[4,28,24,256]{3,2,1,0:T(8,128)(2,1)S(1)}, u32[]{:S(2)}, u32[]{:S(2)}) async-start(bf16[4,28,24,256]{3,2,1,0:T(8,128)(2,1)} %bitcast.14), calls=%async_computation | async-start | bytes 2752512 | tf_op jit(solution)/shard_map/all_to_all | solution.py:303
  9.0 1.6 %copy-start.8 = (f32[2,8]{1,0:T(2,128)S(1)}, f32[2,8]{1,0:T(2,128)}, u32[]{:S(2)}) copy-start(f32[2,8]{1,0:T(2,128)} %param.16) | copy-start | bytes 196
  9.0 2.2 %copy-start.7 = (f32[3,256]{1,0:T(4,128)S(1)}, f32[3,256]{1,0:T(4,128)}, u32[]{:S(2)}) copy-start(f32[3,256]{1,0:T(4,128)} %param.11) | copy-start | bytes 9220
  41.7 1.1 copy-start.1
  54.3 3.9 %copy-start.4 = (bf16[256,768]{1,0:T(8,128)(2,1)S(1)}, bf16[256,768]{1,0:T(8,128)(2,1)}, u32[]{:S(2)}) copy-start(bf16[256,768]{1,0:T(8,128)(2,1)} %param.14) | copy-start | bytes 1179652
  54.3 37.8 %all-to-all-start.1 = ((bf16[16,7,24,256]{3,2,1,0:T(8,128)(2,1)}), bf16[16,7,24,256]{3,2,1,0:T(8,128)(2,1)S(1)}, u32[]{:S(2)}, u32[]{:S(2)}) async-start(bf16[16,7,24,256]{3,2,1,0:T(8,128)(2,1)} %lon_attention.1), calls=%async_computation.1 | async-start | bytes 2752512 | tf_op jit(solution)/shard_map/all_to_all | solution.py:309
  92.1 1.1 copy-start.2
  134.6 7.7 %copy-start = (bf16[4,7,100,256]{3,2,1,0:T(8,128)(2,1)}, bf16[4,7,100,256]{3,2,1,0:T(8,128)(2,1)S(1)}, u32[]{:S(2)}) copy-start(bf16[4,7,100,256]{3,2,1,0:T(8,128)(2,1)S(1)} %all_to_all.15) | copy-start | bytes 4300804
  134.6 7.7 %collective-permute-start = (bf16[2,100,256]{2,1,0:T(8,128)(2,1)S(1)}, bf16[2,100,256]{2,1,0:T(8,128)(2,1)S(1)}, u32[]{:S(2)}, u32[]{:S(2)}) collective-permute-start(bf16[2,100,256]{2,1,0:T(8,128)(2,1)S(1)} %get-tuple-element.6), channel_id=1, source_target_pairs={{0,4},{4,8},{8,12},{12,0},{1,5},{5,9},{9,13},{13,1},{2,6},{6,10},{... | collective-permute-start | bytes 307208 | tf_op jit(solution)/shard_map/ppermute | solution.py:317
  134.6 7.6 %collective-permute-start.1 = (bf16[2,100,256]{2,1,0:T(8,128)(2,1)S(1)}, bf16[2,100,256]{2,1,0:T(8,128)(2,1)S(1)}, u32[]{:S(2)}, u32[]{:S(2)}) collective-permute-start(bf16[2,100,256]{2,1,0:T(8,128)(2,1)S(1)} %get-tuple-element.5), channel_id=1, source_target_pairs={{4,0},{8,4},{12,8},{0,12},{5,1},{9,5},{13,9},{1,13},{6,2},{10,6},{... | collective-permute-start | bytes 307208 | tf_op jit(solution)/shard_map/ppermute | solution.py:318
  142.3 0.6 copy-start.5
  142.3 0.7 copy-start.6

commit v3 on v2

--- a/solution.py
+++ b/solution.py
@@ -82,7 +82,8 @@
     return dot(jnp.concatenate(context, 1), out_w, TN)
 
 
-def lon_kernel(factor_ref, x_ref, gain_ref, wk_ref, wqv_ref, wo_ref, o_ref, state, normed, diag, *, bands, blocks, count):
+def lon_kernel(factor_ref, x_ref, gain_ref, wk_ref, wqv_ref, wo_ref, *rest, bands, blocks, count):
+    *o_refs, state, normed, diag = rest
     cols, rows, features = x_ref.shape
     heads = factor_ref.shape[0]
     width = diag.shape[2]
@@ -122,12 +123,16 @@
             for c, part in enumerate(lanes):
                 state.at[c][at, :] = state.at[c][at, :] + mix[:, part]
 
-    size = o_ref.shape[1]
-    for i in range(bands):
-        for j in range(blocks):
-            at = slice((j * bands + i) * size * rows, (j * bands + i + 1) * size * rows)
-            y = jnp.concatenate([state[c, at, :] for c in range(len(lanes))], 1)
-            o_ref[i * blocks + j] = y.reshape(size, rows, features).astype(jnp.bfloat16)
+    first = 0
+    for o_ref in o_refs:
+        size = o_ref.shape[1]
+        for i in range(bands):
+            for j in range(blocks):
+                start = (j * (cols // blocks) + first + i * size) * rows
+                at = slice(start, start + size * rows)
+                y = jnp.concatenate([state[c, at, :] for c in range(len(lanes))], 1)
+                o_ref[i * blocks + j] = y.reshape(size, rows, features).astype(jnp.bfloat16)
+        first += bands * size
 
 
 def lat_kernel(factor_ref, x_ref, gain_ref, wk_ref, wqv_ref, wo_ref, o_ref, state, diag, *, bands):
@@ -153,38 +158,63 @@
         o_ref[i, 0] = state[first : first + band + 2 * MARGIN, :].astype(jnp.bfloat16)
 
 
-def mixer_kernel(s_ref, before_ref, after_ref, taps_ref, gain_ref, win_ref, wdown_ref, o_ref, wide, normed):
-    cols, tall, features = s_ref.shape
+def mixer_kernel(*refs, strips, filled, tile):
+    count = 1 + max(piece[0] for _, pieces in strips for piece in pieces)
+    inputs = refs[:count]
+    taps_ref, gain_ref, win_ref, wdown_ref = refs[count : count + 4]
+    o_ref, wide, normed, done, sems = refs[count + 4 + filled :]
+    tall, features = inputs[0].shape[1:]
     rows = tall - 2 * MARGIN
-    step = o_ref.shape[0]
     hidden_len = wdown_ref.shape[0]
-    g = pl.program_id(0)
-
-    @pl.when(g == 0)
-    def _():
-        wide[:MARGIN, :tall] = before_ref[...].astype(jnp.float32)
-        wide[MARGIN + cols :, :tall] = after_ref[...].astype(jnp.float32)
-        wide[MARGIN : MARGIN + cols, :tall] = s_ref[...].astype(jnp.float32)
-
-    for c in range(step):
+    outs, at = [], 0
+    for first, pieces in strips:
+        start = at
+        for index, low, high in pieces:
+            wide[at : at + high - low, :tall] = inputs[index][low:high].astype(jnp.float32)
+            at += high - low
+        outs += [(start + c, first + c) for c in range(at - start - 2 * MARGIN)]
+
+    def smooth(n):
+        source = outs[n][0]
         total = None
         for dy in range(KERNEL):
             part = None
             for dx in range(KERNEL):
                 tap = taps_ref[dy * KERNEL + dx : dy * KERNEL + dx + 1, :]
-                term = wide[g * step + c + dx, dy : dy + rows, :] * tap
+                term = wide[source + dx] * tap
                 part = term if part is None else part + term
+            part = part[dy : dy + rows]
             total = part if total is None else total + part
-        normed[c * rows : (c + 1) * rows, :] = layer_norm(total, gain_ref[...]).astype(jnp.bfloat16)
-
-    for c in range(step):
-        line = normed[c * rows : (c + 1) * rows, :]
-        gate = dot(line, win_ref[:, :hidden_len])
-        up = dot(line, win_ref[:, hidden_len:])
+        normed[n * rows : (n + 1) * rows, :] = layer_norm(total, gain_ref[...]).astype(jnp.bfloat16)
+
+    def mix(t, k):
+        line = normed[t * tile * rows : (t + 1) * tile * rows, :]
+        gate = dot(line, win_ref[:, k])
+        up = dot(line, win_ref[:, slice(hidden_len + k.start, hidden_len + k.stop)])
         hidden = (0.5 * gate * (1.0 + jnp.tanh(0.5 * gate)) * up).astype(jnp.bfloat16)
-        update = dot(hidden, wdown_ref[...])
-        kept = wide[g * step + c + MARGIN, MARGIN : MARGIN + rows, :]
-        o_ref[c] = (kept + update).astype(jnp.bfloat16)
+        return dot(hidden, wdown_ref[k, :])
+
+    for n in range(tile):
+        smooth(n)
+    chunk = hidden_len // tile
+    copies = []
+    for t in range(len(outs) // tile):
+        update = None
+        for n in range(tile):
+            term = mix(t, slice(n * chunk, (n + 1) * chunk))
+            update = term if update is None else update + term
+            if (t + 1) * tile + n < len(outs):
+                smooth((t + 1) * tile + n)
+        for n in range(tile):
+            source, target = outs[t * tile + n]
+            kept = wide[source + MARGIN, MARGIN : MARGIN + rows, :]
+            done[t * tile + n] = (kept + update[n * rows : (n + 1) * rows]).astype(jnp.bfloat16)
+            copies.append(
+                pltpu.make_async_copy(done.at[t * tile + n], o_ref.at[target], sems.at[t * tile + n])
+            )
+            copies[-1].start()
+    for copy in copies:
+        copy.wait()
 
 
 def whole(shape):
@@ -201,23 +231,32 @@
 VMEM = pl.BlockSpec(memory_space=pltpu.VMEM)
 
 
-def lon_call(lines, factors, gains, qkv, out_w, bands, blocks, count):
+def cost(cells, length, features, heads):
+    return pl.CostEstimate(
+        flops=2 * cells * features * (4 * features + (heads + 2) * length),
+        bytes_accessed=4 * cells * features,
+        transcendentals=cells * length * heads,
+    )
+
+
+def lon_call(lines, factors, gains, qkv, out_w, bands, blocks, count, sizes):
     all_cols, rows, features = lines.shape
     heads = factors.shape[0]
     wk, wqv = split_weights(qkv, features)
     unroll = next(u for u in (8, 2, 1) if u == 1 or (count % u == 0 and all_cols <= 2 * LANES))
     return pl.pallas_call(
         functools.partial(lon_kernel, bands=bands, blocks=blocks, count=count),
-        out_shape=jax.ShapeDtypeStruct(
-            (bands * blocks, all_cols // (bands * blocks), rows, features), jnp.bfloat16
-        ),
+        out_shape=[
+            jax.ShapeDtypeStruct((bands * blocks, size, rows, features), jnp.bfloat16) for size in sizes
+        ],
         in_specs=[SMEM] + [VMEM] * 5,
-        out_specs=VMEM,
+        out_specs=[VMEM] * len(sizes),
         scratch_shapes=[
             pltpu.VMEM((features // LANES, all_cols * rows, LANES), jnp.float32),
             pltpu.VMEM((features // LANES, all_cols * rows, LANES), jnp.float32),
             pltpu.VMEM((heads * unroll, features, padded(all_cols, LANES)), jnp.bfloat16),
         ],
+        cost_estimate=cost(all_cols * count, all_cols, features, heads),
         name="lon_attention",
     )(factors, lines, gains, wk, wqv, out_w)
 
@@ -245,33 +284,38 @@
             pltpu.VMEM((length + 16, features), jnp.float32),
             pltpu.VMEM((heads, features, length), jnp.bfloat16),
         ],
+        cost_estimate=cost(count * length, length, features, heads),
         name="lat_attention",
     )(factors, columns, gains, wk, wqv, out_w)
 
 
-def mixer_call(block, before, after, taps, gains, win, wdown, steps):
-    cols, tall, features = block.shape
+def mixer_call(inputs, strips, cols, out, taps, gains, win, wdown):
+    _, tall, features = inputs[0].shape
     rows = tall - 2 * MARGIN
+    held = sum(high - low for _, pieces in strips for _, low, high in pieces)
+    count = held - 2 * MARGIN * len(strips)
+    tile = next(n for n in (4, 2, 1) if count % n == 0)
+    some = pl.BlockSpec(memory_space=pl.ANY)
+    before = [] if out is None else [out]
     return pl.pallas_call(
-        mixer_kernel,
-        grid=(steps,),
+        functools.partial(mixer_kernel, strips=strips, filled=len(before), tile=tile),
         out_shape=jax.ShapeDtypeStruct((cols, rows, features), jnp.bfloat16),
-        in_specs=[
-            whole(block.shape),
-            whole(before.shape),
-            whole(after.shape),
-            whole(taps.shape),
-            whole(gains.shape),
-            whole(win.shape),
-            whole(wdown.shape),
-        ],
-        out_specs=pl.BlockSpec((cols // steps, rows, features), lambda g: (g, 0, 0)),
+        in_specs=[VMEM] * (len(inputs) + 4) + [some] * len(before),
+        out_specs=some,
         scratch_shapes=[
-            pltpu.VMEM((cols + 2 * MARGIN, padded(tall, 8), features), jnp.float32),
-            pltpu.VMEM((cols // steps * rows, features), jnp.bfloat16),
-        ],
+            pltpu.VMEM((held, padded(tall, 8), features), jnp.float32),
+            pltpu.VMEM((count * rows, features), jnp.bfloat16),
+            pltpu.VMEM((count, rows, features), jnp.bfloat16),
+            pltpu.SemaphoreType.DMA((count,)),
+        ],
+        input_output_aliases={len(inputs) + 4: 0} if before else {},
+        cost_estimate=pl.CostEstimate(
+            flops=2 * count * rows * features * 3 * wdown.shape[0],
+            bytes_accessed=4 * count * rows * features,
+            transcendentals=count * rows * wdown.shape[0],
+        ),
         name="mixer",
-    )(block, before, after, taps, gains, win, wdown)
+    )(*inputs, taps, gains, win, wdown, *before)
 
 
 def per_device(
@@ -302,22 +346,36 @@
         stacked = jnp.pad(stacked, ((0, 0), (0, 0), (0, tall_rows - sub_rows), (0, 0)))
     lines = lax.all_to_all(stacked, "lon", split_axis=0, concat_axis=0, tiled=True)
     lines = lines.reshape(all_cols, tall_rows, features)
+    sizes = [n for n in (sub_cols - sub_cols // 2, sub_cols // 2) if n]
     first_state = lon_call(
-        lines, factors[0], norm_gains[0:1], lon_qkv, lon_out, bands, blocks, sub_rows
+        lines, factors[0], norm_gains[0:1], lon_qkv, lon_out, bands, blocks, sub_rows, sizes
     )
 
-    columns = lax.all_to_all(first_state, ("lat", "lon"), split_axis=0, concat_axis=0, tiled=True)
-    if tall_rows > sub_rows:
-        columns = jnp.swapaxes(columns[:, :, :sub_rows], 0, 1).reshape(1, sub_cols, all_rows, features)
-    second = lat_call(columns, factors[1], norm_gains[1:2], lat_qkv, lat_out, bands)
-
-    block = lax.all_to_all(second, "lat", split_axis=0, concat_axis=0, tiled=True)
-    block = block.reshape(lon_cols, tall, features)
+    parts = []
+    for size, state in zip(sizes, first_state):
+        columns = lax.all_to_all(state, ("lat", "lon"), split_axis=0, concat_axis=0, tiled=True)
+        if tall_rows > sub_rows:
+            columns = jnp.swapaxes(columns[:, :, :sub_rows], 0, 1).reshape(1, size, all_rows, features)
+        second = lat_call(columns, factors[1], norm_gains[1:2], lat_qkv, lat_out, bands)
+        block = lax.all_to_all(second, "lat", split_axis=0, concat_axis=0, tiled=True)
+        parts.append(block.reshape(bands * size, tall, features))
+
+    left, right = parts
+    shared, rest = left.shape[0], right.shape[0]
     up = [(i, (i + 1) % blocks) for i in range(blocks)]
-    before = lax.ppermute(block[lon_cols - MARGIN :], "lon", up)
-    after = lax.ppermute(block[:MARGIN], "lon", [(j, i) for i, j in up])
-    mixed = mixer_call(block, before, after, conv_taps, norm_gains[2:3], mlp_in, mlp_down, bands)
-    return jnp.transpose(mixed, (1, 0, 2))
+    after = lax.ppermute(left[:MARGIN], "lon", [(j, i) for i, j in up])
+    before = lax.ppermute(right[rest - MARGIN :], "lon", up)
+    mixer = (conv_taps, norm_gains[2:3], mlp_in, mlp_down)
+    edge = 2 * MARGIN
+    out = mixer_call([left], [(MARGIN, [(0, 0, shared)])], lon_cols, None, *mixer)
+    strips = [(shared - MARGIN, [(0, shared - edge, shared), (1, 0, rest)])]
+    out = mixer_call([left, right], strips, lon_cols, out, *mixer)
+    strips = [
+        (0, [(2, 0, MARGIN), (0, 0, edge)]),
+        (lon_cols - MARGIN, [(1, rest - edge, rest), (3, 0, MARGIN)]),
+    ]
+    out = mixer_call([left, right, before, after], strips, lon_cols, out, *mixer)
+    return jnp.transpose(out, (1, 0, 2))
 
 
 def solution(mesh):

time: 161 us -> 157 us (0.975)
  waiting for transfers between devices: 66 us -> 52.2 us
  starting transfers between devices: 14.2 us -> 18.2 us
  Pallas kernels: 48.1 us -> 51.5 us
  local copies, waits for them, and re-layouts: 8.32 us -> 10.3 us
    all_to_all x1 -> x3, waiting for transfers between devices: 32.2 us -> 22.3 us  [the longest x2 11.9 us: per_device(): lax.all_to_all(second, 'lat', split_axis=0, concat_axis=0, tiled=True)]
    all_to_all x1 -> x3, starting transfers between devices: 3.9 us -> 10.6 us  [the longest x2 6.98 us: per_device(): lax.all_to_all(second, 'lat', split_axis=0, concat_axis=0, tiled=True)]
    ppermute x2, waiting for transfers between devices: 3.82 us -> 0.01 us  [the longest x1 0.01 us: per_device(): after = lax.ppermute(left[:MARGIN], 'lon', [(j, i) for i, j in up])]
    ppermute x2, starting transfers between devices: 3.87 us -> 1.17 us  [the longest x1 1.11 us: per_device(): after = lax.ppermute(left[:MARGIN], 'lon', [(j, i) for i, j in up])]
    pallas_call x0 -> x1, local copies, waits for them, and re-layouts: none -> 2.36 us  [lat_call(): pl.pallas_call(functools.partial(lat_kernel, bands=bands), grid=(count,),...]
    pallas_call x1 -> x2, Pallas kernels: 18.7 us -> 20.6 us  [lat_call(): pl.pallas_call(functools.partial(lat_kernel, bands=bands), grid=(count,),...]
    pallas_call x1 -> x3, Pallas kernels: 17.9 us -> 19.4 us  [mixer_call(): pl.pallas_call(functools.partial(mixer_kernel, strips=strips, filled=len(...]
    unnamed x22 -> x24, local copies, waits for them, and re-layouts: 3.24 us -> 2.76 us
  transfers between devices with their start and end apart: 4 -> 6, of which waited for: 3 -> 3; matrix products, arithmetic and copies ran while one was open for 3% -> 4% of each run, Pallas kernels for 0% -> 23%
where the time goes in v3:
time: 157 us; the launch traced here: 156 us
  waiting for transfers between devices  52.2 us (33%)
  Pallas kernels  51.5 us (33%)
  blocking collectives  21.7 us (14%)
  starting transfers between devices  18.2 us (12%)
  local copies, waits for them, and re-layouts  10.3 us (7%)
    all_to_all x1, waiting for transfers between devices, per_device(): lax.all_to_all(stacked, 'lon', split_axis=0, concat_axis=0, tiled=True)  29.9 us
    all_to_all x1, blocking collectives, per_device(): lax.all_to_all(state, ('lat', 'lon'), split_axis=0, concat_axis=0, tiled=...  21.7 us
    pallas_call x2, Pallas kernels, lat_call(): pl.pallas_call(functools.partial(lat_kernel, bands=bands), grid=(count,),...  20.6 us
    pallas_call x3, Pallas kernels, mixer_call(): pl.pallas_call(functools.partial(mixer_kernel, strips=strips, filled=len(...  19.4 us
    all_to_all x2, waiting for transfers between devices, per_device(): lax.all_to_all(second, 'lat', split_axis=0, concat_axis=0, tiled=True)  11.9 us
    pallas_call x1, Pallas kernels, lon_call(): pl.pallas_call(functools.partial(lon_kernel, bands=bands, blocks=blocks,...  11.4 us
    all_to_all x1, waiting for transfers between devices, per_device(): lax.all_to_all(state, ('lat', 'lon'), split_axis=0, concat_axis=0, tiled=...  10.5 us
    all_to_all x2, starting transfers between devices, per_device(): lax.all_to_all(second, 'lat', split_axis=0, concat_axis=0, tiled=True)  6.98 us
  transfers between devices with their start and end apart: 6, of which 3 were waited for; matrix products, arithmetic and copies ran while one was open for 4% of the time, Pallas kernels for 23%

profile of v3, /device:TPU:0, one launch (start us, length us, event | category | flops | bytes accessed | tf_op | source)
XLA Modules:
  0.0 155.8 jit_solution(260577214083438914)
XLA Ops:
  0.0 2.5 %copy.30 = bf16[4,24,28,256]{3,1,2,0:T(8,128)(2,1)} copy(bf16[4,24,28,256]{3,1,0,2:T(8,128)(2,1)} %bitcast.23) | data formatting | bytes 2752512 | tf_op jit(solution)/shard_map/reshape | solution.py:344
  2.5 6.5 %all-to-all-start = ((bf16[4,28,24,256]{3,2,1,0:T(8,128)(2,1)}), bf16[4,28,24,256]{3,2,1,0:T(8,128)(2,1)S(1)}, u32[]{:S(2)}, u32[]{:S(2)}) async-start(bf16[4,28,24,256]{3,2,1,0:T(8,128)(2,1)} %bitcast.15), calls=%async_computation | async-start | bytes 2752512 | tf_op jit(solution)/shard_map/all_to_all | solution.py:347
  9.0 0.7 fusion.1
  9.7 0.1 copy.25
  9.8 0.1 copy.26
  9.9 0.7 maximum_bitcast_fusion.wqv_ref
  10.6 0.6 slice_bitcast_fusion
  11.2 0.6 fusion.2
  11.8 29.9 %all-to-all-done = bf16[4,28,24,256]{3,2,1,0:T(8,128)(2,1)S(1)} async-done(((bf16[4,28,24,256]{3,2,1,0:T(8,128)(2,1)}), bf16[4,28,24,256]{3,2,1,0:T(8,128)(2,1)S(1)}, u32[]{:S(2)}, u32[]{:S(2)}) %all-to-all-start) | async-done | bytes 1376288 | tf_op jit(solution)/shard_map/all_to_all | solution.py:347
  41.7 1.1 copy-done.2
  42.8 11.4 %lon_attention.1 = (bf16[16,4,24,256]{3,2,1,0:T(8,128)(2,1)}, bf16[16,3,24,256]{3,2,1,0:T(8,128)(2,1)}) custom-call(f32[8]{0:T(128)} %get-tuple-element.18.factor_ref, bf16[112,24,256]{2,1,0:T(8,128)(2,1)} %bitcast.24, f32[1,256]{1,0:T(1,128)} %get-tuple-element.16.gain_ref, bf16[256,256]{1,0:T(8,128)(2,1)} %get-tuple-element.13.wk_ref, ...), custom_call_target="tpu_custom_call" | custom-call | flops 2950692864 | bytes 2752512 | tf_op jit(solution)/shard_map/lon_attention/pallas_call | solution.py:247
  54.2 21.7 %all_to_all.25.x_ref = bf16[16,3,24,256]{3,2,1,0:T(8,128)(2,1)} all-to-all(bf16[16,3,24,256]{3,2,1,0:T(8,128)(2,1)} %get-tuple-element.8), channel_id=1, replica_groups=mesh['groups'=2,'lon'=4,'lat'=4] {'lat','lon'}, dimensions={0} | all-to-all | bytes 1179648 | tf_op jit(solution)/shard_map/all_to_all | solution.py:356
  75.9 3.6 %all-to-all-start.1 = ((bf16[16,4,24,256]{3,2,1,0:T(8,128)(2,1)}), bf16[16,4,24,256]{3,2,1,0:T(8,128)(2,1)S(1)}, u32[]{:S(2)}, u32[]{:S(2)}) async-start(bf16[16,4,24,256]{3,2,1,0:T(8,128)(2,1)} %get-tuple-element.7), calls=%async_computation.1 | async-start | bytes 1572864 | tf_op jit(solution)/shard_map/all_to_all | solution.py:356
  79.5 0.7 fusion
  80.2 0.1 copy.27
  80.3 0.1 copy.28
  80.5 0.7 maximum_bitcast_fusion.1.wqv_ref
  81.2 9.1 %lat_attention.3 = bf16[4,3,100,256]{3,2,1,0:T(8,128)(2,1)} custom-call(f32[8]{0:T(128)} %get-tuple-element.19.factor_ref, bf16[16,3,24,256]{3,2,1,0:T(8,128)(2,1)} %all_to_all.25.x_ref, f32[1,256]{1,0:T(1,128)} %get-tuple-element.17.gain_ref, bf16[256,256]{1,0:T(8,128)(2,1)} %get-tuple-element.10.wk_ref, bf16[512,256]{1,0:T(8,128)(2,1)} %maximum_bitcast_fusion.1.wqv_ref, ...), custom_call_target="tpu_custom_call" | custom-call | flops 2868903936 | bytes 1179648 | tf_op jit(solution)/shard_map/lat_attention/pallas_call | solution.py:270
  90.3 10.5 %all-to-all-done.1.x_ref = bf16[16,4,24,256]{3,2,1,0:T(8,128)(2,1)S(1)} async-done(((bf16[16,4,24,256]{3,2,1,0:T(8,128)(2,1)}), bf16[16,4,24,256]{3,2,1,0:T(8,128)(2,1)S(1)}, u32[]{:S(2)}, u32[]{:S(2)}) %all-to-all-start.1) | async-done | bytes 786464 | tf_op jit(solution)/shard_map/all_to_all | solution.py:356
  100.8 3.5 %all-to-all-start.4 = ((bf16[4,3,100,256]{3,2,1,0:T(8,128)(2,1)}), bf16[4,3,100,256]{3,2,1,0:T(8,128)(2,1)S(1)}, u32[]{:S(2)}, u32[]{:S(2)}) async-start(bf16[4,3,100,256]{3,2,1,0:T(8,128)(2,1)} %lat_attention.3), calls=%async_computation.4 | async-start | bytes 1277952 | tf_op jit(solution)/shard_map/all_to_all | solution.py:360
  104.2 11.5 %lat_attention.2 = bf16[4,4,100,256]{3,2,1,0:T(8,128)(2,1)} custom-call(f32[8]{0:T(128)} %get-tuple-element.19.factor_ref, bf16[16,4,24,256]{3,2,1,0:T(8,128)(2,1)} %copy-done.3, f32[1,256]{1,0:T(1,128)} %get-tuple-element.17.gain_ref, bf16[256,256]{1,0:T(8,128)(2,1)} %get-tuple-element.10.wk_ref, bf16[512,256]{1,0:T(8,128)(2,1)} %maximum_bitcast_fusion.1.wqv_ref, ...), custom_call_target="tpu_custom_call" | custom-call | flops 3825205248 | bytes 1572864 | tf_op jit(solution)/shard_map/lat_attention/pallas_call | solution.py:270
  115.8 2.4 %copy.23 = bf16[4,4,100,256]{3,1,2,0:T(4,128)(2,1)} copy(bf16[4,4,100,256]{3,2,1,0:T(8,128)(2,1)} %lat_attention.2) | data formatting | bytes 1638400 | tf_op jit(solution)/shard_map/lat_attention/pallas_call | solution.py:270
  118.1 3.5 %all-to-all-start.2 = ((bf16[4,4,100,256]{3,1,2,0:T(4,128)(2,1)}), bf16[4,4,100,256]{3,1,2,0:T(4,128)(2,1)S(1)}, u32[]{:S(2)}, u32[]{:S(2)}) async-start(bf16[4,4,100,256]{3,1,2,0:T(4,128)(2,1)} %copy.23), calls=%async_computation.2 | async-start | bytes 1638400 | tf_op jit(solution)/shard_map/all_to_all | solution.py:360
  121.7 0.1 collective-permute-start
  121.7 11.9 %all-to-all-done.2 = bf16[4,4,100,256]{3,1,2,0:T(4,128)(2,1)S(1)} async-done(((bf16[4,4,100,256]{3,1,2,0:T(4,128)(2,1)}), bf16[4,4,100,256]{3,1,2,0:T(4,128)(2,1)S(1)}, u32[]{:S(2)}, u32[]{:S(2)}) %all-to-all-start.2) | async-done | bytes 819232 | tf_op jit(solution)/shard_map/all_to_all | solution.py:360
  133.6 0.1 copy.24
  133.7 1.1 collective-permute-start.1
  134.8 7.3 %mixer.3.refs_6_ = bf16[28,96,256]{2,1,0:T(8,128)(2,1)} custom-call(bf16[16,100,256]{2,1,0:T(8,128)(2,1)} %bitcast.17, f32[25,256]{1,0:T(8,128)} %refs_4_.5, f32[1,256]{1,0:T(1,128)} %get-tuple-element.15.refs_2_.refs_3_.refs_5_, bf16[256,2048]{1,0:T(8,128)(2,1)} %refs_6_.1, bf16[1024,256]{1,0:T(8,128)(2,1)} %refs_7_.1), custom_call_target="tpu_custom_call" | custom-call | flops 1811939328 | bytes 1179648 | tf_op jit(solution)/shard_map/mixer/pallas_call | solution.py:300
  142.2 7.5 %mixer.4.refs_8_ = bf16[28,96,256]{2,1,0:T(8,128)(2,1)} custom-call(bf16[16,100,256]{2,1,0:T(8,128)(2,1)} %bitcast.18, bf16[12,100,256]{2,1,0:T(8,128)(2,1)} %bitcast.21, f32[25,256]{1,0:T(8,128)} %refs_4_.5, f32[1,256]{1,0:T(1,128)} %get-tuple-element.15.refs_2_.refs_3_.refs_5_, bf16[256,2048]{1,0:T(8,128)(2,1)} %refs_6_.1, ...), custom_call_target="tpu_custom_call", output_to_operand_aliasing={{}: (6, {})} | custom-call | flops 1811939328 | bytes 1179648 | tf_op jit(solution)/shard_map/mixer/pallas_call | solution.py:300
  149.8 0.6 copy-done.6
  150.4 0.6 copy-done.7
  151.0 4.6 %mixer.5 = bf16[28,96,256]{2,1,0:T(8,128)(2,1)} custom-call(bf16[16,100,256]{2,1,0:T(8,128)(2,1)} %bitcast.19, bf16[12,100,256]{2,1,0:T(8,128)(2,1)} %bitcast.22, bf16[2,100,256]{2,1,0:T(8,128)(2,1)} %copy-done.6, bf16[2,100,256]{2,1,0:T(8,128)(2,1)} %copy-done.7, f32[25,256]{1,0:T(8,128)} %refs_4_.5, ...), custom_call_target="tpu_custom_call", output_to_operand_aliasing={{}: (8, {})} | custom-call | flops 603979776 | bytes 393216 | tf_op jit(solution)/shard_map/mixer/pallas_call | solution.py:300
  (23 shorter events, 0.1 us)
Async XLA Ops:
  2.5 6.5 %copy-start.4 = (bf16[256,768]{1,0:T(8,128)(2,1)S(1)}, bf16[256,768]{1,0:T(8,128)(2,1)}, u32[]{:S(2)}) copy-start(bf16[256,768]{1,0:T(8,128)(2,1)} %param.12) | copy-start | bytes 1179652
  2.5 39.2 %all-to-all-start = ((bf16[4,28,24,256]{3,2,1,0:T(8,128)(2,1)}), bf16[4,28,24,256]{3,2,1,0:T(8,128)(2,1)S(1)}, u32[]{:S(2)}, u32[]{:S(2)}) async-start(bf16[4,28,24,256]{3,2,1,0:T(8,128)(2,1)} %bitcast.15), calls=%async_computation | async-start | bytes 2752512 | tf_op jit(solution)/shard_map/all_to_all | solution.py:347
  9.0 1.6 %copy-start.9 = (f32[2,8]{1,0:T(2,128)S(1)}, f32[2,8]{1,0:T(2,128)}, u32[]{:S(2)}) copy-start(f32[2,8]{1,0:T(2,128)} %param.16) | copy-start | bytes 196
  9.0 2.2 %copy-start.8 = (f32[3,256]{1,0:T(4,128)S(1)}, f32[3,256]{1,0:T(4,128)}, u32[]{:S(2)}) copy-start(f32[3,256]{1,0:T(4,128)} %param.11) | copy-start | bytes 9220
  41.7 1.1 copy-start.2
  54.2 25.3 %copy-start.5 = (bf16[256,768]{1,0:T(8,128)(2,1)S(1)}, bf16[256,768]{1,0:T(8,128)(2,1)}, u32[]{:S(2)}) copy-start(bf16[256,768]{1,0:T(8,128)(2,1)} %param.14) | copy-start | bytes 1179652
  75.9 24.8 %all-to-all-start.1 = ((bf16[16,4,24,256]{3,2,1,0:T(8,128)(2,1)}), bf16[16,4,24,256]{3,2,1,0:T(8,128)(2,1)S(1)}, u32[]{:S(2)}, u32[]{:S(2)}) async-start(bf16[16,4,24,256]{3,2,1,0:T(8,128)(2,1)} %get-tuple-element.7), calls=%async_computation.1 | async-start | bytes 1572864 | tf_op jit(solution)/shard_map/all_to_all | solution.py:356
  100.7 3.5 %copy-start.3 = (bf16[16,4,24,256]{3,2,1,0:T(8,128)(2,1)}, bf16[16,4,24,256]{3,2,1,0:T(8,128)(2,1)S(1)}, u32[]{:S(2)}) copy-start(bf16[16,4,24,256]{3,2,1,0:T(8,128)(2,1)S(1)} %all-to-all-done.1.x_ref) | copy-start | bytes 2359300
  100.8 17.4 %all-to-all-start.4 = ((bf16[4,3,100,256]{3,2,1,0:T(8,128)(2,1)}), bf16[4,3,100,256]{3,2,1,0:T(8,128)(2,1)S(1)}, u32[]{:S(2)}, u32[]{:S(2)}) async-start(bf16[4,3,100,256]{3,2,1,0:T(8,128)(2,1)} %lat_attention.3), calls=%async_computation.4 | async-start | bytes 1277952 | tf_op jit(solution)/shard_map/all_to_all | solution.py:360
  118.1 15.6 %copy-start.1 = (bf16[4,3,100,256]{3,2,1,0:T(8,128)(2,1)}, bf16[4,3,100,256]{3,2,1,0:T(8,128)(2,1)S(1)}, u32[]{:S(2)}) copy-start(bf16[4,3,100,256]{3,2,1,0:T(8,128)(2,1)S(1)} %all-to-all-done.4) | copy-start | bytes 1843204
  118.1 15.4 %all-to-all-start.2 = ((bf16[4,4,100,256]{3,1,2,0:T(4,128)(2,1)}), bf16[4,4,100,256]{3,1,2,0:T(4,128)(2,1)S(1)}, u32[]{:S(2)}, u32[]{:S(2)}) async-start(bf16[4,4,100,256]{3,1,2,0:T(4,128)(2,1)} %copy.23), calls=%async_computation.2 | async-start | bytes 1638400 | tf_op jit(solution)/shard_map/all_to_all | solution.py:360
  121.7 28.1 %collective-permute-start = (bf16[2,100,256]{2,1,0:T(8,128)(2,1)S(1)}, bf16[2,100,256]{2,1,0:T(8,128)(2,1)S(1)}, u32[]{:S(2)}, u32[]{:S(2)}) collective-permute-start(bf16[2,100,256]{2,1,0:T(8,128)(2,1)S(1)} %slice.57), channel_id=1, source_target_pairs={{0,4},{4,8},{8,12},{12,0},{1,5},{5,9},{9,13},{13,1},{2,6},{6,10},{... | collective-permute-start | bytes 307208 | tf_op jit(solution)/shard_map/ppermute | solution.py:367
  133.7 1.1 copy-start
  133.7 16.0 %collective-permute-start.1 = (bf16[2,100,256]{2,1,0:T(8,128)(2,1)S(1)}, bf16[2,100,256]{2,1,0:T(8,128)(2,1)S(1)}, u32[]{:S(2)}, u32[]{:S(2)}) collective-permute-start(bf16[2,100,256]{2,1,0:T(8,128)(2,1)S(1)} %slice.58), channel_id=1, source_target_pairs={{4,0},{8,4},{12,8},{0,12},{5,1},{9,5},{13,9},{1,13},{6,2},{10,6},{... | collective-permute-start | bytes 307208 | tf_op jit(solution)/shard_map/ppermute | solution.py:366
  149.7 0.6 copy-start.6
  150.4 0.6 copy-start.7

commit v4 on v3

--- a/solution.py
+++ b/solution.py
@@ -155,7 +155,7 @@
     band = length // bands
     for i in range(bands):
         first = 8 + i * band - MARGIN
-        o_ref[i, 0] = state[first : first + band + 2 * MARGIN, :].astype(jnp.bfloat16)
+        o_ref[i, 0] = state[first : first + o_ref.shape[2], :].astype(jnp.bfloat16)
 
 
 def mixer_kernel(*refs, strips, filled, tile):
@@ -164,13 +164,13 @@
     taps_ref, gain_ref, win_ref, wdown_ref = refs[count : count + 4]
     o_ref, wide, normed, done, sems = refs[count + 4 + filled :]
     tall, features = inputs[0].shape[1:]
-    rows = tall - 2 * MARGIN
+    rows = o_ref.shape[1]
     hidden_len = wdown_ref.shape[0]
     outs, at = [], 0
     for first, pieces in strips:
         start = at
         for index, low, high in pieces:
-            wide[at : at + high - low, :tall] = inputs[index][low:high].astype(jnp.float32)
+            wide[at : at + high - low] = inputs[index][low:high].astype(jnp.float32)
             at += high - low
         outs += [(start + c, first + c) for c in range(at - start - 2 * MARGIN)]
 
@@ -265,7 +265,7 @@
     sources, count, rows, features = columns.shape
     heads = factors.shape[0]
     length = sources * rows
-    tall = length // bands + 2 * MARGIN
+    tall = padded(length // bands + 2 * MARGIN, 8)
     wk, wqv = split_weights(qkv, features)
     return pl.pallas_call(
         functools.partial(lat_kernel, bands=bands),
@@ -281,7 +281,7 @@
         ],
         out_specs=pl.BlockSpec((bands, 1, tall, features), lambda k: (0, k, 0, 0)),
         scratch_shapes=[
-            pltpu.VMEM((length + 16, features), jnp.float32),
+            pltpu.VMEM((length + 8 + tall - length // bands, features), jnp.float32),
             pltpu.VMEM((heads, features, length), jnp.bfloat16),
         ],
         cost_estimate=cost(count * length, length, features, heads),
@@ -289,9 +289,8 @@
     )(factors, columns, gains, wk, wqv, out_w)
 
 
-def mixer_call(inputs, strips, cols, out, taps, gains, win, wdown):
+def mixer_call(inputs, strips, cols, rows, out, taps, gains, win, wdown):
     _, tall, features = inputs[0].shape
-    rows = tall - 2 * MARGIN
     held = sum(high - low for _, pieces in strips for _, low, high in pieces)
     count = held - 2 * MARGIN * len(strips)
     tile = next(n for n in (4, 2, 1) if count % n == 0)
@@ -303,7 +302,7 @@
         in_specs=[VMEM] * (len(inputs) + 4) + [some] * len(before),
         out_specs=some,
         scratch_shapes=[
-            pltpu.VMEM((held, padded(tall, 8), features), jnp.float32),
+            pltpu.VMEM((held, tall, features), jnp.float32),
             pltpu.VMEM((count * rows, features), jnp.bfloat16),
             pltpu.VMEM((count, rows, features), jnp.bfloat16),
             pltpu.SemaphoreType.DMA((count,)),
@@ -338,7 +337,7 @@
     sub_cols = lon_cols // bands
     all_cols = lon_cols * blocks
     all_rows = lat_rows * bands
-    tall = lat_rows + 2 * MARGIN
+    tall = padded(lat_rows + 2 * MARGIN, 8)
     factors = logit_scales * LOG2E
 
     stacked = jnp.transpose(fields.reshape(blocks, sub_rows, lon_cols, features), (0, 2, 1, 3))
@@ -351,30 +350,45 @@
         lines, factors[0], norm_gains[0:1], lon_qkv, lon_out, bands, blocks, sub_rows, sizes
     )
 
-    parts = []
-    for size, state in zip(sizes, first_state):
+    def to_columns(state):
         columns = lax.all_to_all(state, ("lat", "lon"), split_axis=0, concat_axis=0, tiled=True)
         if tall_rows > sub_rows:
-            columns = jnp.swapaxes(columns[:, :, :sub_rows], 0, 1).reshape(1, size, all_rows, features)
-        second = lat_call(columns, factors[1], norm_gains[1:2], lat_qkv, lat_out, bands)
-        block = lax.all_to_all(second, "lat", split_axis=0, concat_axis=0, tiled=True)
-        parts.append(block.reshape(bands * size, tall, features))
-
-    left, right = parts
+            columns = jnp.swapaxes(columns[:, :, :sub_rows], 0, 1)
+            columns = columns.reshape(1, columns.shape[0], all_rows, features)
+        return columns
+
+    def to_block(state):
+        block = lax.all_to_all(state, "lat", split_axis=0, concat_axis=0, tiled=True)
+        return block.reshape(-1, tall, features)
+
+    def attend(columns):
+        return lat_call(columns, factors[1], norm_gains[1:2], lat_qkv, lat_out, bands)
+
+    near, far = first_state
+    near = to_columns(near)
+    near, far = lax.optimization_barrier((near, far))
+    far = to_columns(far)
+    near = attend(near)
+    near, far = lax.optimization_barrier((near, far))
+    left = to_block(near)
+    far = attend(far)
+    left, far = lax.optimization_barrier((left, far))
+    right = to_block(far)
+
     shared, rest = left.shape[0], right.shape[0]
     up = [(i, (i + 1) % blocks) for i in range(blocks)]
     after = lax.ppermute(left[:MARGIN], "lon", [(j, i) for i, j in up])
     before = lax.ppermute(right[rest - MARGIN :], "lon", up)
     mixer = (conv_taps, norm_gains[2:3], mlp_in, mlp_down)
     edge = 2 * MARGIN
-    out = mixer_call([left], [(MARGIN, [(0, 0, shared)])], lon_cols, None, *mixer)
+    out = mixer_call([left], [(MARGIN, [(0, 0, shared)])], lon_cols, lat_rows, None, *mixer)
     strips = [(shared - MARGIN, [(0, shared - edge, shared), (1, 0, rest)])]
-    out = mixer_call([left, right], strips, lon_cols, out, *mixer)
+    out = mixer_call([left, right], strips, lon_cols, lat_rows, out, *mixer)
     strips = [
         (0, [(2, 0, MARGIN), (0, 0, edge)]),
         (lon_cols - MARGIN, [(1, rest - edge, rest), (3, 0, MARGIN)]),
     ]
-    out = mixer_call([left, right, before, after], strips, lon_cols, out, *mixer)
+    out = mixer_call([left, right, before, after], strips, lon_cols, lat_rows, out, *mixer)
     return jnp.transpose(out, (1, 0, 2))
 
 

time: 157 us -> 145 us (0.924)
  waiting for transfers between devices: 52.2 us -> 38.4 us
  blocking collectives: 21.7 us -> 25.7 us
  local copies, waits for them, and re-layouts: 10.3 us -> 8.32 us
    all_to_all x3, waiting for transfers between devices: 22.3 us -> 8.45 us  [the longest x2 4.63 us: to_block(): lax.all_to_all(state, 'lat', split_axis=0, concat_axis=0, tiled=True)]
    all_to_all x1, blocking collectives: 21.7 us -> 25.7 us  [to_columns(): lax.all_to_all(state, ('lat', 'lon'), split_axis=0, concat_axis=0, tiled=...]
    pallas_call x1 -> x0, local copies, waits for them, and re-layouts: 2.36 us -> none  [lat_call(): pl.pallas_call(functools.partial(lat_kernel, bands=bands), grid=(count,),...]
  transfers between devices with their start and end apart: 6 -> 6, of which waited for: 3 -> 4; matrix products, arithmetic and copies ran while one was open for 4% -> 3% of each run, Pallas kernels for 23% -> 25%
where the time goes in v4:
time: 145 us; the launch traced here: 144 us
  Pallas kernels  51.5 us (36%)
  waiting for transfers between devices  38.4 us (26%)
  blocking collectives  25.7 us (18%)
  starting transfers between devices  18.5 us (13%)
  local copies, waits for them, and re-layouts  8.32 us (6%)
  other arithmetic  1.46 us (1%)
    all_to_all x1, waiting for transfers between devices, per_device(): lax.all_to_all(stacked, 'lon', split_axis=0, concat_axis=0, tiled=True)  30 us
    all_to_all x1, blocking collectives, to_columns(): lax.all_to_all(state, ('lat', 'lon'), split_axis=0, concat_axis=0, tiled=...  25.7 us
    pallas_call x2, Pallas kernels, lat_call(): pl.pallas_call(functools.partial(lat_kernel, bands=bands), grid=(count,),...  20.7 us
    pallas_call x3, Pallas kernels, mixer_call(): pl.pallas_call(functools.partial(mixer_kernel, strips=strips, filled=len(...  19.4 us
    pallas_call x1, Pallas kernels, lon_call(): pl.pallas_call(functools.partial(lon_kernel, bands=bands, blocks=blocks,...  11.4 us
    all_to_all x2, starting transfers between devices, to_block(): lax.all_to_all(state, 'lat', split_axis=0, concat_axis=0, tiled=True)  6.98 us
    all_to_all x1, starting transfers between devices, per_device(): lax.all_to_all(stacked, 'lon', split_axis=0, concat_axis=0, tiled=True)  6.48 us
    all_to_all x2, waiting for transfers between devices, to_block(): lax.all_to_all(state, 'lat', split_axis=0, concat_axis=0, tiled=True)  4.63 us
  transfers between devices with their start and end apart: 6, of which 4 were waited for; matrix products, arithmetic and copies ran while one was open for 3% of the time, Pallas kernels for 25%

profile of v4, /device:TPU:0, one launch (start us, length us, event | category | flops | bytes accessed | tf_op | source)
XLA Modules:
  0.0 144.2 jit_solution(16413980989761633047)
XLA Ops:
  0.0 2.5 %copy.23 = bf16[4,24,28,256]{3,1,2,0:T(8,128)(2,1)} copy(bf16[4,24,28,256]{3,1,0,2:T(8,128)(2,1)} %bitcast.23) | data formatting | bytes 2752512 | tf_op jit(solution)/shard_map/reshape | solution.py:343
  2.5 6.5 %all-to-all-start = ((bf16[4,28,24,256]{3,2,1,0:T(8,128)(2,1)}), bf16[4,28,24,256]{3,2,1,0:T(8,128)(2,1)S(1)}, u32[]{:S(2)}, u32[]{:S(2)}) async-start(bf16[4,28,24,256]{3,2,1,0:T(8,128)(2,1)} %bitcast.15), calls=%async_computation | async-start | bytes 2752512 | tf_op jit(solution)/shard_map/all_to_all | solution.py:346
  9.0 0.7 fusion.1
  9.7 0.1 copy.18
  9.8 0.1 copy.19
  9.9 0.7 maximum_bitcast_fusion.wqv_ref
  10.6 0.5 slice_bitcast_fusion
  11.2 0.6 fusion.2
  11.8 30.0 %all-to-all-done = bf16[4,28,24,256]{3,2,1,0:T(8,128)(2,1)S(1)} async-done(((bf16[4,28,24,256]{3,2,1,0:T(8,128)(2,1)}), bf16[4,28,24,256]{3,2,1,0:T(8,128)(2,1)S(1)}, u32[]{:S(2)}, u32[]{:S(2)}) %all-to-all-start) | async-done | bytes 1376288 | tf_op jit(solution)/shard_map/all_to_all | solution.py:346
  41.7 1.1 copy-done.2
  42.8 11.4 %lon_attention.1 = (bf16[16,4,24,256]{3,2,1,0:T(8,128)(2,1)}, bf16[16,3,24,256]{3,2,1,0:T(8,128)(2,1)}) custom-call(f32[8]{0:T(128)} %get-tuple-element.30.factor_ref, bf16[112,24,256]{2,1,0:T(8,128)(2,1)} %bitcast.24, f32[1,256]{1,0:T(1,128)} %get-tuple-element.28.gain_ref, bf16[256,256]{1,0:T(8,128)(2,1)} %get-tuple-element.25.wk_ref, ...), custom_call_target="tpu_custom_call" | custom-call | flops 2950692864 | bytes 2752512 | tf_op jit(solution)/shard_map/lon_attention/pallas_call | solution.py:247
  54.2 25.7 %all_to_all.25.x_ref = bf16[16,4,24,256]{3,2,1,0:T(8,128)(2,1)} all-to-all(bf16[16,4,24,256]{3,2,1,0:T(8,128)(2,1)} %get-tuple-element.13), channel_id=1, replica_groups=mesh['groups'=2,'lon'=4,'lat'=4] {'lat','lon'}, dimensions={0} | all-to-all | bytes 1572864 | tf_op jit(solution)/shard_map/all_to_all | solution.py:354
  79.9 3.6 %all-to-all-start.2 = ((bf16[16,3,24,256]{3,2,1,0:T(8,128)(2,1)}), bf16[16,3,24,256]{3,2,1,0:T(8,128)(2,1)S(1)}, u32[]{:S(2)}, u32[]{:S(2)}) async-start(bf16[16,3,24,256]{3,2,1,0:T(8,128)(2,1)} %get-tuple-element.16), calls=%async_computation.2 | async-start | bytes 1179648 | tf_op jit(solution)/shard_map/all_to_all | solution.py:354
  83.5 0.7 fusion
  84.2 0.1 copy.20
  84.3 0.1 copy.21
  84.4 0.7 maximum_bitcast_fusion.1.wqv_ref
  85.1 11.5 %lat_attention.2 = bf16[4,4,104,256]{3,2,1,0:T(8,128)(2,1)} custom-call(f32[8]{0:T(128)} %get-tuple-element.31.factor_ref, bf16[16,4,24,256]{3,2,1,0:T(8,128)(2,1)} %all_to_all.25.x_ref, f32[1,256]{1,0:T(1,128)} %get-tuple-element.29.gain_ref, bf16[256,256]{1,0:T(8,128)(2,1)} %get-tuple-element.22.wk_ref, bf16[512,256]{1,0:T(8,128)(2,1)} %maximum_bitcast_fusion.1.wqv_ref, ...), custom_call_target="tpu_custom_call" | custom-call | flops 3825205248 | bytes 1572864 | tf_op jit(solution)/shard_map/lat_attention/pallas_call | solution.py:270
  96.6 3.8 %all-to-all-done.2.x_ref = bf16[16,3,24,256]{3,2,1,0:T(8,128)(2,1)S(1)} async-done(((bf16[16,3,24,256]{3,2,1,0:T(8,128)(2,1)}), bf16[16,3,24,256]{3,2,1,0:T(8,128)(2,1)S(1)}, u32[]{:S(2)}, u32[]{:S(2)}) %all-to-all-start.2) | async-done | bytes 589856 | tf_op jit(solution)/shard_map/all_to_all | solution.py:354
  100.4 3.5 %all-to-all-start.3 = ((bf16[4,4,104,256]{3,2,1,0:T(8,128)(2,1)}), bf16[4,4,104,256]{3,2,1,0:T(8,128)(2,1)S(1)}, u32[]{:S(2)}, u32[]{:S(2)}) async-start(bf16[4,4,104,256]{3,2,1,0:T(8,128)(2,1)} %lat_attention.2), calls=%async_computation.3 | async-start | bytes 1703936 | tf_op jit(solution)/shard_map/all_to_all | solution.py:361
  104.0 9.2 %lat_attention.3 = bf16[4,3,104,256]{3,2,1,0:T(8,128)(2,1)} custom-call(f32[8]{0:T(128)} %get-tuple-element.31.factor_ref, bf16[16,3,24,256]{3,2,1,0:T(8,128)(2,1)} %copy-done.3, f32[1,256]{1,0:T(1,128)} %get-tuple-element.29.gain_ref, bf16[256,256]{1,0:T(8,128)(2,1)} %get-tuple-element.22.wk_ref, bf16[512,256]{1,0:T(8,128)(2,1)} %maximum_bitcast_fusion.1.wqv_ref, ...), custom_call_target="tpu_custom_call" | custom-call | flops 2868903936 | bytes 1179648 | tf_op jit(solution)/shard_map/lat_attention/pallas_call | solution.py:270
  113.1 3.1 %all-to-all-done.3 = bf16[4,4,104,256]{3,2,1,0:T(8,128)(2,1)S(1)} async-done(((bf16[4,4,104,256]{3,2,1,0:T(8,128)(2,1)}), bf16[4,4,104,256]{3,2,1,0:T(8,128)(2,1)S(1)}, u32[]{:S(2)}, u32[]{:S(2)}) %all-to-all-start.3) | async-done | bytes 852000 | tf_op jit(solution)/shard_map/all_to_all | solution.py:361
  116.2 3.5 %all-to-all-start.4 = ((bf16[4,3,104,256]{3,2,1,0:T(8,128)(2,1)}), bf16[4,3,104,256]{3,2,1,0:T(8,128)(2,1)S(1)}, u32[]{:S(2)}, u32[]{:S(2)}) async-start(bf16[4,3,104,256]{3,2,1,0:T(8,128)(2,1)} %lat_attention.3), calls=%async_computation.4 | async-start | bytes 1277952 | tf_op jit(solution)/shard_map/all_to_all | solution.py:361
  119.8 1.2 collective-permute-start.1
  120.9 7.3 %mixer.3.refs_6_ = bf16[28,96,256]{2,1,0:T(8,128)(2,1)} custom-call(bf16[16,104,256]{2,1,0:T(8,128)(2,1)} %bitcast.17, f32[25,256]{1,0:T(8,128)} %refs_4_.5, f32[1,256]{1,0:T(1,128)} %get-tuple-element.27.refs_2_.refs_3_.refs_5_, bf16[256,2048]{1,0:T(8,128)(2,1)} %refs_6_.1, bf16[1024,256]{1,0:T(8,128)(2,1)} %refs_7_.1), custom_call_target="tpu_custom_call" | custom-call | flops 1811939328 | bytes 1179648 | tf_op jit(solution)/shard_map/mixer/pallas_call | solution.py:299
  128.2 1.5 %all-to-all-done.4 = bf16[4,3,104,256]{3,2,1,0:T(8,128)(2,1)S(1)} async-done(((bf16[4,3,104,256]{3,2,1,0:T(8,128)(2,1)}), bf16[4,3,104,256]{3,2,1,0:T(8,128)(2,1)S(1)}, u32[]{:S(2)}, u32[]{:S(2)}) %all-to-all-start.4) | async-done | bytes 639008 | tf_op jit(solution)/shard_map/all_to_all | solution.py:361
  129.8 0.3 collective-permute-start
  130.0 0.6 copy-done.1
  130.6 7.5 %mixer.4.refs_8_ = bf16[28,96,256]{2,1,0:T(8,128)(2,1)} custom-call(bf16[16,104,256]{2,1,0:T(8,128)(2,1)} %bitcast.18, bf16[12,104,256]{2,1,0:T(8,128)(2,1)} %bitcast.21, f32[25,256]{1,0:T(8,128)} %refs_4_.5, f32[1,256]{1,0:T(1,128)} %get-tuple-element.27.refs_2_.refs_3_.refs_5_, bf16[256,2048]{1,0:T(8,128)(2,1)} %refs_6_.1, ...), custom_call_target="tpu_custom_call", output_to_operand_aliasing={{}: (6, {})} | custom-call | flops 1811939328 | bytes 1179648 | tf_op jit(solution)/shard_map/mixer/pallas_call | solution.py:299
  138.2 0.6 copy-done.6
  138.8 0.6 copy-done.7
  139.4 4.6 %mixer.5 = bf16[28,96,256]{2,1,0:T(8,128)(2,1)} custom-call(bf16[16,104,256]{2,1,0:T(8,128)(2,1)} %bitcast.19, bf16[12,104,256]{2,1,0:T(8,128)(2,1)} %bitcast.22, bf16[2,104,256]{2,1,0:T(8,128)(2,1)} %copy-done.7, bf16[2,104,256]{2,1,0:T(8,128)(2,1)} %copy-done.6, f32[25,256]{1,0:T(8,128)} %refs_4_.5, ...), custom_call_target="tpu_custom_call", output_to_operand_aliasing={{}: (8, {})} | custom-call | flops 603979776 | bytes 393216 | tf_op jit(solution)/shard_map/mixer/pallas_call | solution.py:299
  (21 shorter events, 0.1 us)
Async XLA Ops:
  2.5 6.5 %copy-start.4 = (bf16[256,768]{1,0:T(8,128)(2,1)S(1)}, bf16[256,768]{1,0:T(8,128)(2,1)}, u32[]{:S(2)}) copy-start(bf16[256,768]{1,0:T(8,128)(2,1)} %param.12) | copy-start | bytes 1179652
  2.5 39.2 %all-to-all-start = ((bf16[4,28,24,256]{3,2,1,0:T(8,128)(2,1)}), bf16[4,28,24,256]{3,2,1,0:T(8,128)(2,1)S(1)}, u32[]{:S(2)}, u32[]{:S(2)}) async-start(bf16[4,28,24,256]{3,2,1,0:T(8,128)(2,1)} %bitcast.15), calls=%async_computation | async-start | bytes 2752512 | tf_op jit(solution)/shard_map/all_to_all | solution.py:346
  9.0 1.6 %copy-start.9 = (f32[2,8]{1,0:T(2,128)S(1)}, f32[2,8]{1,0:T(2,128)}, u32[]{:S(2)}) copy-start(f32[2,8]{1,0:T(2,128)} %param.16) | copy-start | bytes 196
  9.0 2.2 %copy-start.8 = (f32[3,256]{1,0:T(4,128)S(1)}, f32[3,256]{1,0:T(4,128)}, u32[]{:S(2)}) copy-start(f32[3,256]{1,0:T(4,128)} %param.11) | copy-start | bytes 9220
  41.7 1.1 copy-start.2
  54.2 29.3 %copy-start.5 = (bf16[256,768]{1,0:T(8,128)(2,1)S(1)}, bf16[256,768]{1,0:T(8,128)(2,1)}, u32[]{:S(2)}) copy-start(bf16[256,768]{1,0:T(8,128)(2,1)} %param.14) | copy-start | bytes 1179652
  79.9 20.5 %all-to-all-start.2 = ((bf16[16,3,24,256]{3,2,1,0:T(8,128)(2,1)}), bf16[16,3,24,256]{3,2,1,0:T(8,128)(2,1)S(1)}, u32[]{:S(2)}, u32[]{:S(2)}) async-start(bf16[16,3,24,256]{3,2,1,0:T(8,128)(2,1)} %get-tuple-element.16), calls=%async_computation.2 | async-start | bytes 1179648 | tf_op jit(solution)/shard_map/all_to_all | solution.py:354
  100.4 3.5 %copy-start.3 = (bf16[16,3,24,256]{3,2,1,0:T(8,128)(2,1)}, bf16[16,3,24,256]{3,2,1,0:T(8,128)(2,1)S(1)}, u32[]{:S(2)}) copy-start(bf16[16,3,24,256]{3,2,1,0:T(8,128)(2,1)S(1)} %all-to-all-done.2.x_ref) | copy-start | bytes 1769476
  100.4 15.8 %all-to-all-start.3 = ((bf16[4,4,104,256]{3,2,1,0:T(8,128)(2,1)}), bf16[4,4,104,256]{3,2,1,0:T(8,128)(2,1)S(1)}, u32[]{:S(2)}, u32[]{:S(2)}) async-start(bf16[4,4,104,256]{3,2,1,0:T(8,128)(2,1)} %lat_attention.2), calls=%async_computation.3 | async-start | bytes 1703936 | tf_op jit(solution)/shard_map/all_to_all | solution.py:361
  116.2 4.7 %copy-start = (bf16[4,4,104,256]{3,2,1,0:T(8,128)(2,1)}, bf16[4,4,104,256]{3,2,1,0:T(8,128)(2,1)S(1)}, u32[]{:S(2)}) copy-start(bf16[4,4,104,256]{3,2,1,0:T(8,128)(2,1)S(1)} %all-to-all-done.3) | copy-start | bytes 2555908
  116.2 13.5 %all-to-all-start.4 = ((bf16[4,3,104,256]{3,2,1,0:T(8,128)(2,1)}), bf16[4,3,104,256]{3,2,1,0:T(8,128)(2,1)S(1)}, u32[]{:S(2)}, u32[]{:S(2)}) async-start(bf16[4,3,104,256]{3,2,1,0:T(8,128)(2,1)} %lat_attention.3), calls=%async_computation.4 | async-start | bytes 1277952 | tf_op jit(solution)/shard_map/all_to_all | solution.py:361
  119.8 18.4 %collective-permute-start.1 = (bf16[2,104,256]{2,1,0:T(8,128)(2,1)S(1)}, bf16[2,104,256]{2,1,0:T(8,128)(2,1)S(1)}, u32[]{:S(2)}, u32[]{:S(2)}) collective-permute-start(bf16[2,104,256]{2,1,0:T(8,128)(2,1)S(1)} %slice.55), channel_id=1, source_target_pairs={{4,0},{8,4},{12,8},{0,12},{5,1},{9,5},{13,9},{1,13},{6,2},{10,6},{... | collective-permute-start | bytes 319496 | tf_op jit(solution)/shard_map/ppermute | solution.py:380
  129.7 0.9 copy-start.1
  129.8 8.4 %collective-permute-start = (bf16[2,104,256]{2,1,0:T(8,128)(2,1)S(1)}, bf16[2,104,256]{2,1,0:T(8,128)(2,1)S(1)}, u32[]{:S(2)}, u32[]{:S(2)}) collective-permute-start(bf16[2,104,256]{2,1,0:T(8,128)(2,1)S(1)} %slice.57), channel_id=1, source_target_pairs={{0,4},{4,8},{8,12},{12,0},{1,5},{5,9},{9,13},{13,1},{2,6},{6,10},{... | collective-permute-start | bytes 319496 | tf_op jit(solution)/shard_map/ppermute | solution.py:381
  138.1 0.6 copy-start.6
  138.8 0.6 copy-start.7
